TPU v7x, 1024 devices: a whole 8x8x8 slice. The times are simulated.
1024 devices in a mesh: dp: 16 (over x, core), expert: 64 (over z, y).
Axes of the slice: x: 8, y: 8, z: 8, core: 2. Of those that a mesh axis runs over, the one named last changes fastest.
Arguments:
- out_grad: bfloat16 [8192, 4096], P('expert', 'dp'), may hold values from -6 to 6
- layer_input: bfloat16 [8192, 4096], P('expert', 'dp'), may hold values from -0.59765625 to 0.59765625
- expert_ids: int32 [8192, 8], P('expert'), may hold values from 0 to 63, as said below
- selected_logits: float32 [8192, 8], P('expert'), may hold values from -6 to 6
- saved_hidden: bfloat16 [64, 64, 32, 768], P(None, 'expert'), may hold values from -6 to 6
- saved_output: bfloat16 [64, 64, 32, 4096], P(None, 'expert', None, 'dp'), may hold values from -0.375 to 0.375
- down_weight: bfloat16 [64, 4096, 768], P('expert', 'dp'), may hold values from -0.21875 to 0.21875
Outputs:
- hidden_grad: bfloat16 [64, 64, 32, 768], P(None, 'expert', 'dp')
- down_grad: float32 [64, 4096, 768], P('expert', 'dp')
- logit_grad: float32 [8192, 8], P('expert')
- router_grad: float32 [64, 4096], P('expert', 'dp')
Inputs may be any that keep to these rules, and one draw needn't show every extreme that they name: `expert_ids`: each row names 8 different experts. In the rows of one device no expert is named more than 32 times, and some experts are named exactly 32 times by the rows of every device.
All inputs are finite; a program needn't handle non-finite values.
Results may differ from a plain program's by a relative error of at most 0.0057.
Values may be sent and summed in bfloat16 or wider, within the bound.
No kernel may reach another device: no remote copies, remote signals or barrier semaphores. Data moves between devices by JAX's collectives and lax.ppermute only.
A program may use at most 64 MiB of HBM per device.

v0:
```python
import jax
import jax.numpy as jnp
from jax import lax
from jax.sharding import PartitionSpec as P


def in_one_piece(arrays, axis, split_dim, concat_dim, along):
    columns = [a.reshape(*a.shape[:along], -1) for a in arrays]
    both = jnp.concatenate(columns, axis=along)
    result, at, outs = (
        lax.all_to_all(both, axis, split_axis=split_dim, concat_axis=concat_dim, tiled=True),
        0,
        [],
    )
    for a, column in zip(arrays, columns):
        section = result[..., at : at + column.shape[along]]
        outs.append(section.reshape(*section.shape[:along], *a.shape[along:]))
        at += column.shape[along]
    return tuple(outs)


def from_everyone(x, axis):
    copies = jnp.broadcast_to(x, (lax.axis_size(axis), *x.shape))
    return lax.all_to_all(copies, axis, split_axis=0, concat_axis=0, tiled=True)


def taken_together(x, axis):
    return from_everyone(x, axis).sum(axis=0)


def in_blocks(x, dim, length):
    lengths = x.shape
    tiles = x.reshape(*lengths[:dim], length, lengths[dim] // length, *lengths[dim + 1 :])
    return jnp.moveaxis(tiles, dim, 0)


def sum_at_owner(x, axis, dim):
    length = lax.axis_size(axis)
    tiles = lax.all_to_all(in_blocks(x, dim, length), axis, 0, 0, tiled=True)
    return jnp.sum(tiles, axis=0)


def body(
    out_grad, layer_input, expert_ids, selected_logits, saved_hidden, saved_output, down_weight
):
    per_expert = down_weight.shape[0]
    capacity = saved_hidden.shape[2]
    n_expert = lax.axis_size("expert")
    experts_all = n_expert * per_expert
    token_count = out_grad.shape[0]
    pick_count = expert_ids.shape[1]
    dcols = out_grad.shape[1]
    slots_dev = token_count * pick_count
    buffer_rows = experts_all * capacity
    routed = expert_ids.reshape(slots_dev)
    positions = jnp.arange(slots_dev, dtype=jnp.int32)
    same = routed[:, None] == routed[None, :]
    earlier = positions[None, :] < positions[:, None]
    slot_index = jnp.sum(jnp.logical_and(same, earlier), axis=1)
    target = routed * capacity + slot_index
    raised = jnp.exp(selected_logits)
    gating = raised / jnp.sum(raised, axis=-1, keepdims=True)
    gate_rounded = gating.astype(jnp.bfloat16)
    placement = jnp.arange(buffer_rows, dtype=jnp.int32)[:, None] == target[None, :]
    per_token = jnp.any(placement.reshape(buffer_rows, token_count, pick_count), axis=2).astype(
        jnp.bfloat16
    )
    send_rows = jnp.dot(per_token, out_grad, preferred_element_type=jnp.float32).astype(
        jnp.bfloat16
    )
    send_gates = jnp.dot(
        placement.astype(jnp.bfloat16),
        gate_rounded.reshape(slots_dev),
        preferred_element_type=jnp.float32,
    ).astype(jnp.bfloat16)
    send_rows = send_rows.reshape(n_expert, per_expert, capacity, dcols)
    send_gates = send_gates.reshape(n_expert, per_expert, capacity)
    got_rows, got_gates = in_one_piece((send_rows, send_gates), "expert", 0, 0, 3)
    scaled_rows = got_gates[..., None] * got_rows
    delta_part = jnp.einsum(
        "slcd,slcd->slc", got_rows, saved_output, preferred_element_type=jnp.float32
    )
    returned = lax.all_to_all(delta_part, "expert", split_axis=0, concat_axis=0, tiled=True)
    gate_part = returned.reshape(buffer_rows)[target].reshape(token_count, pick_count)
    gate_delta = taken_together(gate_part, "dp")
    logit_grad = gating * (gate_delta - jnp.sum(gating * gate_delta, axis=-1, keepdims=True))
    summed = lax.psum_scatter(
        jnp.einsum("slcd,ldf->cslf", scaled_rows, down_weight, preferred_element_type=jnp.float32),
        "dp",
        scatter_dimension=0,
        tiled=True,
    )
    hidden_grad = jnp.transpose(summed, (1, 2, 0, 3)).astype(jnp.bfloat16)
    down_grad = jnp.einsum(
        "slcd,slcf->ldf", scaled_rows, saved_hidden, preferred_element_type=jnp.float32
    )
    onehot = (
        expert_ids[:, :, None] == jnp.arange(experts_all, dtype=jnp.int32)[None, None, :]
    ).astype(jnp.float32)
    weights_by_expert = jnp.einsum("tk,tke->et", logit_grad, onehot)
    router_term = jnp.dot(
        weights_by_expert, layer_input.astype(jnp.float32), precision=lax.Precision.HIGHEST
    )
    router_grad = sum_at_owner(router_term, "expert", 0)
    return (hidden_grad, down_grad, logit_grad, router_grad)


def solution(mesh):
    placed = (
        P("expert", "dp"),
        P("expert", "dp"),
        P("expert", None),
        P("expert", None),
        P(None, "expert", None, None),
        P(None, "expert", None, "dp"),
        P("expert", "dp", None),
    )
    return jax.shard_map(
        body,
        mesh=mesh,
        in_specs=placed,
        out_specs=(
            P(None, "expert", "dp", None),
            P("expert", "dp", None),
            P("expert", None),
            P("expert", "dp"),
        ),
        check_vma=False,
    )
```

profile of v0, /device:TPU:15, one launch (start us, length us, event | category | flops | bytes accessed | tf_op | source)
XLA Modules:
  0.0 178.9 jit_solution(11954504776635641026)
XLA Ops:
  7.2 0.0 copy-start
  7.2 0.0 reduce-scatter.2.cloned.1.call-start
  7.2 0.9 copy.39
  8.2 0.1 eq.49
  8.3 0.5 convert_reduce_fusion
  8.8 0.1 reduce_sum.52
  8.9 0.7 exponential_reduce_fusion
  9.6 0.7 fusion.17
  10.3 0.1 copy.42
  10.4 0.1 reshape.115
  10.5 1.5 fusion.1
  12.1 7.4 %fusion = pred[2048,128]{1,0:T(8,128)(4,1)S(1)} fusion(s32[128,8]{0,1:T(8,128)S(1)} %copy.41), kind=kLoop, calls=%fused_computation.3 | loop fusion | flops 3932160 | bytes 266240 | tf_op jit(solution)/shard_map/reduce_or | solution.py:65
  19.5 1.8 %reshape_reshape.4 = bf16[64,1,32,1]{3,2,1,0:T(8,128)(2,1)} reshape(bf16[2048]{0:T(1024)(128)(2,1)S(1)} %convert_element_type.25) | data formatting | bytes 8192 | tf_op jit(solution)/shard_map/reshape;reshape | solution.py:8
  21.3 1.3 convolution_convert_fusion
  22.6 1.3 pad_maximum_fusion
  23.8 62.0 %all_to_all.20 = bf16[64,1,32,257]{3,2,1,0:T(8,128)(2,1)S(1)} all-to-all(bf16[64,1,32,257]{3,2,1,0:T(8,128)(2,1)S(1)} %pad_maximum_fusion), channel_id=1, replica_groups=mesh['dp'=16,'expert'=64] {'expert'}, dimensions={0} | all-to-all | bytes 2105344 | tf_op jit(solution)/shard_map/all_to_all | solution.py:11
  85.8 0.0 copy-start.1
  85.8 1.1 copy-done.1
  87.0 0.9 slice.10
  87.9 1.5 copy.60
  89.4 2.4 %convolution_bitcast_fusion = f32[32,64,1,768]{3,0,1,2:T(8,128)S(1)} fusion(bf16[64,1,32,257]{3,2,1,0:T(8,128)(2,1)} %copy-done.1, bf16[64,32]{1,0:T(8,128)(2,1)S(1)} %bitcast.51, bf16[1,256,768]{2,1,0:T(8,128)(2,1)} %param.13), kind=kOutput, calls=%fused_computation.11 | convolution fusion | flops 805830656 | bytes 7737344 | tf_op jit(solution)/shard_map/slcd,ldf->cslf/dot_general | solution.py:88
  91.7 6.3 %copy.47 = f32[32,64,1,768]{3,1,2,0:T(8,128)} copy(f32[32,64,1,768]{3,0,1,2:T(8,128)S(1)} %convolution_bitcast_fusion) | data formatting | bytes 12582912 | tf_op jit(solution)/shard_map/slcd,ldf->cslf/transpose | solution.py:88
  98.0 0.0 reduce-scatter.2.cloned.1.call-update
  98.0 0.1 mul.48
  98.2 0.0 copy-start.3
  98.2 2.5 %fusion.6 = f32[64,32]{1,0:T(8,128)} fusion(bf16[64,1,32,256]{3,2,1,0:T(8,128)(2,1)} %param.12, bf16[64,1,32,257]{3,2,1,0:T(8,128)(2,1)} %copy-done.1), kind=kLoop, calls=%fused_computation.14 | loop fusion | flops 2095104 | bytes 2105344 | tf_op jit(solution)/shard_map/slcd,slcd->slc/dot_general | solution.py:80
  100.7 0.0 copy-start.2
  100.7 8.7 %all-to-all-start.1 = ((f32[64,1,32]{2,1,0:T(1,128)}), f32[64,1,32]{2,1,0:T(1,128)S(1)}, u32[]{:S(2)}, u32[]{:S(2)}) async-start(f32[64,1,32]{2,1,0:T(1,128)} %bitcast.16), calls=%async_computation.2 | async-start | bytes 65536 | tf_op jit(solution)/shard_map/all_to_all | solution.py:83
  109.4 10.8 %all-to-all-done.1 = f32[64,1,32]{2,1,0:T(1,128)S(1)} async-done(((f32[64,1,32]{2,1,0:T(1,128)}), f32[64,1,32]{2,1,0:T(1,128)S(1)}, u32[]{:S(2)}, u32[]{:S(2)}) %all-to-all-start.1) | async-done | bytes 8224 | tf_op jit(solution)/shard_map/all_to_all | solution.py:83
  120.1 0.5 broadcast.44
  120.7 0.7 reduce.6
  121.4 0.1 reshape.104
  121.5 6.1 %gather_fusion = f32[1024]{0:T(1024)S(1)} fusion(f32[2048]{0:T(1024)S(1)} %reshape.104, s32[1024]{0:T(1024)S(1)} %broadcast_clamp_fusion), kind=kCustom, calls=%fused_computation | custom fusion | bytes 12288 | tf_op jit(solution)/shard_map/gather | solution.py:84
  127.6 0.1 reshape.105
  127.8 15.6 %all_to_all.21 = f32[16,128,8]{1,2,0:T(8,128)S(1)} all-to-all(f32[16,128,8]{1,2,0:T(8,128)S(1)} %broadcast_in_dim.2), channel_id=1, replica_groups=mesh['dp'=16,'expert'=64] {'dp'}, dimensions={0} | all-to-all | bytes 131072 | tf_op jit(solution)/shard_map/all_to_all | solution.py:24
  143.4 0.0 copy-done.3
  143.5 0.0 copy-start.4
  143.5 0.1 copy.56
  143.6 0.4 fusion.14
  144.0 0.0 copy-done.2
  144.0 0.2 convolution_bitcast_fusion.1
  144.2 0.7 copy.50
  144.9 4.6 %all-to-all-start.3 = ((f32[64,1,256]{2,1,0:T(1,128)}), f32[64,1,256]{2,1,0:T(1,128)S(1)}, u32[]{:S(2)}, u32[]{:S(2)}) async-start(f32[64,1,256]{2,1,0:T(1,128)} %copy.50), calls=%async_computation.4 | async-start | bytes 131072 | tf_op jit(solution)/shard_map/all_to_all | solution.py:39
  149.5 0.0 copy-done
  149.6 3.4 %fusion.7 = f32[1,256,768]{2,1,0:T(8,128)} fusion(bf16[64,1,32,768]{3,2,1,0:T(8,128)(2,1)S(1)} %copy-done, bf16[64,1,32,257]{3,2,1,0:T(8,128)(2,1)} %copy-done.1, bf16[64,32]{1,0:T(8,128)(2,1)S(1)} %bitcast.52), kind=kOutput, calls=%fused_computation.16 | convolution fusion | flops 805830656 | bytes 4984832 | tf_op jit(solution)/shard_map/slcd,slcf->ldf/dot_general | solution.py:94
  153.0 0.0 copy-done.4
  153.0 7.7 %all-to-all-done.3 = f32[64,1,256]{2,1,0:T(1,128)S(1)} async-done(((f32[64,1,256]{2,1,0:T(1,128)}), f32[64,1,256]{2,1,0:T(1,128)S(1)}, u32[]{:S(2)}, u32[]{:S(2)}) %all-to-all-start.3) | async-done | bytes 65568 | tf_op jit(solution)/shard_map/all_to_all | solution.py:39
  160.7 0.7 reduce_sum.57
  161.3 8.8 %reduce-scatter.2.cloned.1.call-done = f32[2,64,1,768]{3,1,2,0:T(8,128)} async-done(((f32[32,64,1,768]{3,1,2,0:T(8,128)}), f32[2,64,1,768]{3,1,2,0:T(8,128)}) %reduce-scatter.2.cloned.1.call-update) | async-done | bytes 393232 | tf_op jit(solution)/shard_map/reduce_scatter | solution.py:87
  170.2 1.0 convert_bitcast_fusion
  171.2 0.9 copy.51
  (11 shorter events, 0.2 us)
Async XLA Ops:
  7.2 142.4 %copy-start = (bf16[64,1,32,768]{3,2,1,0:T(8,128)(2,1)S(1)}, bf16[64,1,32,768]{3,2,1,0:T(8,128)(2,1)}, u32[]{:S(2)}) copy-start(bf16[64,1,32,768]{3,2,1,0:T(8,128)(2,1)} %param.11) | copy-start | bytes 9437188
  7.2 163.0 %reduce-scatter.2.cloned.1.call-start = ((), (), s32[]{:S(2)}) async-start(), calls=%async_computation.5 | async-start | bytes 6684672 | tf_op jit(solution)/shard_map/reduce_scatter | solution.py:87
  85.8 1.1 copy-start.1
  98.2 45.3 %copy-start.3 = (f32[128,8]{0,1:T(8,128)S(1)}, f32[128,8]{0,1:T(8,128)}, u32[]{:S(2)}) copy-start(f32[128,8]{0,1:T(8,128)} %param.10) | copy-start | bytes 12292
  100.7 43.3 %copy-start.2 = (bf16[128,256]{1,0:T(8,128)(2,1)S(1)}, bf16[128,256]{1,0:T(8,128)(2,1)}, u32[]{:S(2)}) copy-start(bf16[128,256]{1,0:T(8,128)(2,1)} %param.8) | copy-start | bytes 196612
  100.7 19.5 %all-to-all-start.1 = ((f32[64,1,32]{2,1,0:T(1,128)}), f32[64,1,32]{2,1,0:T(1,128)S(1)}, u32[]{:S(2)}, u32[]{:S(2)}) async-start(f32[64,1,32]{2,1,0:T(1,128)} %bitcast.16), calls=%async_computation.2 | async-start | bytes 65536 | tf_op jit(solution)/shard_map/all_to_all | solution.py:83
  143.5 9.5 %copy-start.4 = (f32[128,8]{0,1:T(8,128)}, f32[128,8]{0,1:T(8,128)S(1)}, u32[]{:S(2)}) copy-start(f32[128,8]{0,1:T(8,128)S(1)} %subtract_multiply_fusion) | copy-start | bytes 12292
  144.9 15.7 %all-to-all-start.3 = ((f32[64,1,256]{2,1,0:T(1,128)}), f32[64,1,256]{2,1,0:T(1,128)S(1)}, u32[]{:S(2)}, u32[]{:S(2)}) async-start(f32[64,1,256]{2,1,0:T(1,128)} %copy.50), calls=%async_computation.4 | async-start | bytes 131072 | tf_op jit(solution)/shard_map/all_to_all | solution.py:39
Sparse Core Ops, SparseCore 0:
  98.2 71.9 reduce-scatter.1
where the time goes:
time: 180 us; the launch traced here: 179 us
  blocking collectives  77.6 us (43%)
  waiting for transfers between devices  27.3 us (15%)
  local copies, waits for them, and re-layouts  21.7 us (12%)
  other arithmetic  15.6 us (9%)
  between operations  14.2 us (8%)
  starting transfers between devices  13.3 us (7%)
  matrix products  9.09 us (5%)
    all_to_all x1, blocking collectives, in_one_piece(): lax.all_to_all(both, axis, split_axis=split_dim, concat_axis=concat_dim,...  62 us
    all_to_all x1, blocking collectives, from_everyone(): return lax.all_to_all(copies, axis, split_axis=0, concat_axis=0, tiled=True)  15.6 us
    all_to_all x1, waiting for transfers between devices, body(): lax.all_to_all(delta_part, 'expert', split_axis=0, concat_axis=0, tiled=T...  10.8 us
    reduce_scatter x1, waiting for transfers between devices, body(): lax.psum_scatter(jnp.einsum('slcd,ldf->cslf', scaled_rows, down_weight, p...  8.85 us
    all_to_all x1, starting transfers between devices, body(): lax.all_to_all(delta_part, 'expert', split_axis=0, concat_axis=0, tiled=T...  8.65 us
    all_to_all x1, waiting for transfers between devices, sum_at_owner(): tiles = lax.all_to_all(in_blocks(x, dim, length), axis, 0, 0, tiled=True)  7.68 us
    reduce_or x1, other arithmetic, body(): jnp.any(placement.reshape(buffer_rows, token_count, pick_count), axis=2)  7.43 us
    transpose x1, local copies, waits for them, and re-layouts, body(): jnp.einsum('slcd,ldf->cslf', scaled_rows, down_weight, preferred_element_...  6.3 us
  transfers between devices with their start and end apart: 3, of which 3 were waited for; matrix products, arithmetic and copies ran while one was open for 9% of the time, Pallas kernels for 0%

commit v1 on v0

v1 whole, which is shorter than its diff:
```python
import jax
import jax.numpy as jnp
from jax import lax
from jax.experimental import pallas as pl
from jax.experimental.pallas import tpu as pltpu
from jax.sharding import PartitionSpec as P

BF = jnp.bfloat16
F32 = jnp.float32


def dot(a, b):
    return jnp.dot(a, b, preferred_element_type=F32)


def exact_dot(a, b):
    return jnp.dot(a, b, precision=lax.Precision.HIGHEST, preferred_element_type=F32)


def place_kernel(capacity, ids_ref, logits_ref, rows_ref, send_ref, key_ref, gating_ref):
    top, tokens = ids_ref.shape
    experts = key_ref.shape[0]
    ids = ids_ref[...]
    raised = jnp.exp(logits_ref[...])
    gating = raised / jnp.sum(raised, axis=0, keepdims=True)
    gating_ref[...] = gating
    rounded = gating.astype(BF).astype(F32)
    expert = lax.broadcasted_iota(jnp.int32, (experts, tokens), 0)
    named = jnp.zeros((experts, tokens), F32)
    gate = jnp.zeros((experts, tokens), F32)
    for k in range(top):
        here = ids[k : k + 1, :] == expert
        named = jnp.where(here, 1.0, named)
        gate = jnp.where(here, rounded[k : k + 1, :], gate)
    first = lax.broadcasted_iota(jnp.int32, (tokens, tokens), 0)
    later = lax.broadcasted_iota(jnp.int32, (tokens, tokens), 1)
    before = jnp.where(first < later, 1.0, 0.0).astype(BF)
    slot = dot(named.astype(BF), before)
    key = jnp.where(named > 0.0, slot, -1.0).astype(jnp.int32)
    key_ref[...] = key
    shape = (experts, capacity, tokens)
    slots = lax.broadcasted_iota(jnp.int32, shape, 1)
    chosen = jnp.where(key[:, None, :] == slots, gate[:, None, :], 0.0)
    chosen = chosen.reshape(experts * capacity, tokens).astype(BF)
    send_ref[...] = dot(chosen, rows_ref[...]).astype(BF)


def pick_kernel(back_ref, ids_ref, key_ref, out_ref):
    experts, capacity = back_ref.shape
    top, tokens = ids_ref.shape
    key = key_ref[...]
    back = back_ref[...]
    dense = jnp.zeros((experts, tokens), F32)
    for c in range(capacity):
        dense = jnp.where(key == c, back[:, c : c + 1], dense)
    expert = lax.broadcasted_iota(jnp.int32, (experts, tokens), 0)
    for k in range(top):
        here = ids_ref[k : k + 1, :] == expert
        out_ref[k : k + 1, :] = jnp.sum(jnp.where(here, dense, 0.0), axis=0, keepdims=True)


def grad_kernel(parts_ref, gating_ref, ids_ref, input_ref, logit_ref, term_ref):
    top, tokens = ids_ref.shape
    experts = term_ref.shape[0]
    gating = gating_ref[...]
    total = jnp.sum(parts_ref[...], axis=0)
    delta = total / gating.astype(BF).astype(F32)
    grad = gating * (delta - jnp.sum(gating * delta, axis=0, keepdims=True))
    logit_ref[...] = grad
    expert = lax.broadcasted_iota(jnp.int32, (experts, tokens), 0)
    spread = jnp.zeros((experts, tokens), F32)
    for k in range(top):
        spread = jnp.where(ids_ref[k : k + 1, :] == expert, grad[k : k + 1, :], spread)
    term_ref[...] = exact_dot(spread, input_ref[...].astype(F32))


def whole(shape, dtype):
    return jax.ShapeDtypeStruct(shape, dtype)


def body(
    out_grad, layer_input, expert_ids, selected_logits, saved_hidden, saved_output, down_weight
):
    n_expert = lax.axis_size("expert")
    n_dp = lax.axis_size("dp")
    tokens, top = expert_ids.shape
    dcols = out_grad.shape[1]
    capacity, ff = saved_hidden.shape[2:]
    experts = n_expert
    ids = expert_ids.T
    logits = selected_logits.T
    send, key, gating = pl.pallas_call(
        lambda *refs: place_kernel(capacity, *refs),
        out_shape=(
            whole((experts * capacity, dcols), BF),
            whole((experts, tokens), jnp.int32),
            whole((top, tokens), F32),
        ),
        name="place",
    )(ids, logits, out_grad)
    got = lax.all_to_all(
        send.reshape(n_expert, capacity, dcols), "expert", split_axis=0, concat_axis=0, tiled=True
    )
    outputs = saved_output.reshape(n_expert, capacity, dcols)
    hidden = saved_hidden.reshape(n_expert * capacity, ff)
    weight = down_weight.reshape(dcols, ff)
    back = jnp.sum(got.astype(F32) * outputs.astype(F32), axis=-1)
    by_slot = lax.optimization_barrier(jnp.swapaxes(got, 0, 1))
    part = dot(by_slot.reshape(capacity * n_expert, dcols), weight)
    summed = lax.psum_scatter(
        part.reshape(capacity, n_expert, ff), "dp", scatter_dimension=0, tiled=True
    )
    hidden_grad = jnp.swapaxes(summed, 0, 1).astype(BF).reshape(n_expert, 1, capacity // n_dp, ff)
    down_grad = lax.dot_general(
        got.reshape(n_expert * capacity, dcols),
        hidden,
        (((0,), (0,)), ((), ())),
        preferred_element_type=F32,
    )
    returned = lax.all_to_all(back[:, None, :], "expert", 0, 0, tiled=True)
    picked = pl.pallas_call(pick_kernel, out_shape=whole((top, tokens), F32), name="pick")(
        returned.reshape(n_expert, capacity), ids, key
    )
    copies = jnp.broadcast_to(picked, (n_dp, top, tokens))
    parts = lax.all_to_all(copies, "dp", 0, 0, tiled=True)
    logit_grad, term = pl.pallas_call(
        grad_kernel,
        out_shape=(whole((top, tokens), F32), whole((experts, dcols), F32)),
        name="grads",
    )(parts, gating, ids, layer_input)
    tiles = lax.all_to_all(term.reshape(n_expert, 1, dcols), "expert", 0, 0, tiled=True)
    router_grad = jnp.sum(tiles, axis=0)
    return (hidden_grad, down_grad.reshape(1, dcols, ff), logit_grad.T, router_grad)


def solution(mesh):
    placed = (
        P("expert", "dp"),
        P("expert", "dp"),
        P("expert", None),
        P("expert", None),
        P(None, "expert", None, None),
        P(None, "expert", None, "dp"),
        P("expert", "dp", None),
    )
    return jax.shard_map(
        body,
        mesh=mesh,
        in_specs=placed,
        out_specs=(
            P(None, "expert", "dp", None),
            P("expert", "dp", None),
            P("expert", None),
            P("expert", "dp"),
        ),
        check_vma=False,
    )
```

time: 180 us -> 148 us (0.82)
  local copies, waits for them, and re-layouts: 21.7 us -> 4.11 us
  other arithmetic: 15.6 us -> 3.57 us
  starting transfers between devices: 13.3 us -> 4.63 us
  blocking collectives: 77.6 us -> 84.7 us
  Pallas kernels: 0 us -> 6.15 us
  waiting for transfers between devices: 27.3 us -> 21.2 us
    all_to_all x2 -> x1, waiting for transfers between devices: 18.5 us -> 8.02 us  [body(): lax.all_to_all(term.reshape(n_expert, 1, dcols), 'expert', 0, 0, tiled=True)]
    all_to_all x2 -> x1, starting transfers between devices: 13.3 us -> 4.6 us  [body(): lax.all_to_all(term.reshape(n_expert, 1, dcols), 'expert', 0, 0, tiled=True)]
    reduce_or x1 -> x0, other arithmetic: 7.43 us -> none  [body(): jnp.any(placement.reshape(buffer_rows, token_count, pick_count), axis=2)]
    all_to_all x2 -> x3, blocking collectives: 77.6 us -> 84.7 us  [the longest x1 50.6 us: body(): lax.all_to_all(send.reshape(n_expert, capacity, dcols), 'expert', split_a...]
    transpose x1 -> x0, local copies, waits for them, and re-layouts: 6.3 us -> none  [body(): jnp.einsum('slcd,ldf->cslf', scaled_rows, down_weight, preferred_element_...]
    pallas_call x0 -> x3, Pallas kernels: none -> 6.15 us  [the longest x1 2.58 us: body(): pl.pallas_call(lambda *refs: place_kernel(capacity, *refs), out_shape=(wh...]
    gather x1 -> x0, local copies, waits for them, and re-layouts: 6.15 us -> none  [body(): returned.reshape(buffer_rows)[target].reshape(token_count, pick_count)]
    reduce_scatter x1, waiting for transfers between devices: 8.85 us -> 13.2 us  [body(): lax.psum_scatter(part.reshape(capacity, n_expert, ff), 'dp', scatter_dime...]
  transfers between devices with their start and end apart: 3 -> 2, of which waited for: 3 -> 2; matrix products, arithmetic and copies ran while one was open for 9% -> 5% of each run, Pallas kernels for 0% -> 2%
where the time goes in v1:
time: 148 us; the launch traced here: 147 us
  blocking collectives  84.7 us (57%)
  waiting for transfers between devices  21.2 us (14%)
  between operations  14.1 us (10%)
  matrix products  8.65 us (6%)
  Pallas kernels  6.15 us (4%)
  starting transfers between devices  4.63 us (3%)
  local copies, waits for them, and re-layouts  4.11 us (3%)
  other arithmetic  3.57 us (2%)
    all_to_all x1, blocking collectives, body(): lax.all_to_all(send.reshape(n_expert, capacity, dcols), 'expert', split_a...  50.6 us
    all_to_all x1, blocking collectives, body(): returned = lax.all_to_all(back[:, None, :], 'expert', 0, 0, tiled=True)  18.6 us
    all_to_all x1, blocking collectives, body(): parts = lax.all_to_all(copies, 'dp', 0, 0, tiled=True)  15.4 us
    reduce_scatter x1, waiting for transfers between devices, body(): lax.psum_scatter(part.reshape(capacity, n_expert, ff), 'dp', scatter_dime...  13.2 us
    all_to_all x1, waiting for transfers between devices, body(): lax.all_to_all(term.reshape(n_expert, 1, dcols), 'expert', 0, 0, tiled=True)  8.02 us
    dot_general x1, matrix products, dot(): return jnp.dot(a, b, preferred_element_type=F32)  5.53 us
    all_to_all x1, starting transfers between devices, body(): lax.all_to_all(term.reshape(n_expert, 1, dcols), 'expert', 0, 0, tiled=True)  4.6 us
    dot_general x1, matrix products, body(): lax.dot_general(got.reshape(n_expert * capacity, dcols), hidden, (((0,),...  3.12 us
  transfers between devices with their start and end apart: 2, of which 2 were waited for; matrix products, arithmetic and copies ran while one was open for 5% of the time, Pallas kernels for 2%

profile of v1, /device:TPU:15, one launch (start us, length us, event | category | flops | bytes accessed | tf_op | source)
XLA Modules:
  0.0 147.1 jit_solution(8810425366404162952)
XLA Ops:
  7.2 0.0 copy-start
  7.2 0.0 reduce-scatter.2.cloned.1.call-start
  7.2 2.6 %place.1 = (bf16[2048,256]{1,0:T(8,128)(2,1)}, s32[64,128]{1,0:T(8,128)}, f32[8,128]{1,0:T(8,128)}) custom-call(s32[8,128]{1,0:T(8,128)} %bitcast.33, f32[8,128]{1,0:T(8,128)} %bitcast.36, bf16[128,256]{1,0:T(8,128)(2,1)} %refs_2_.1), custom_call_target="tpu_custom_call" | custom-call | tf_op jit(solution)/shard_map/place/pallas_call | solution.py:92
  9.8 50.6 %all_to_all.20 = bf16[64,32,256]{2,1,0:T(8,128)(2,1)S(1)} all-to-all(bf16[64,32,256]{2,1,0:T(8,128)(2,1)} %bitcast.29), channel_id=1, replica_groups=mesh['dp'=16,'expert'=64] {'expert'}, dimensions={0} | all-to-all | bytes 2097152 | tf_op jit(solution)/shard_map/all_to_all | solution.py:101
  60.4 0.0 copy-start.1
  60.4 1.0 copy-done.1
  61.4 5.5 %fusion.1 = f32[32,64,768]{2,1,0:T(8,128)} fusion(bf16[32,64,256]{2,0,1:T(8,128)(2,1)S(1)} %bitcast.27, bf16[1,256,768]{2,1,0:T(8,128)(2,1)} %param.13), kind=kOutput, calls=%fused_computation.3 | convolution fusion | flops 805306368 | bytes 7733248 | tf_op jit(solution)/shard_map/dot_general | solution.py:13
  66.9 0.0 reduce-scatter.2.cloned.1.call-update
  67.0 1.9 %fusion = f32[64,32]{1,0:T(8,128)S(1)} fusion(bf16[64,32,256]{2,1,0:T(8,128)(2,1)} %copy-done.1, bf16[64,1,32,256]{3,2,1,0:T(8,128)(2,1)} %param.12), kind=kLoop, calls=%fused_computation.1 | loop fusion | flops 2095104 | bytes 2105344 | tf_op jit(solution)/shard_map/reduce_sum | solution.py:107
  68.9 18.6 %all_to_all.21 = f32[64,1,32]{2,1,0:T(1,128)} all-to-all(f32[64,1,32]{2,1,0:T(1,128)S(1)} %bitcast.30), channel_id=1, replica_groups=mesh['dp'=16,'expert'=64] {'expert'}, dimensions={0} | all-to-all | bytes 16384 | tf_op jit(solution)/shard_map/all_to_all | solution.py:120
  87.5 1.8 %pick.1 = f32[8,128]{1,0:T(8,128)} custom-call(f32[64,32]{1,0:T(8,128)} %bitcast.31, s32[8,128]{1,0:T(8,128)} %bitcast.34, s32[64,128]{1,0:T(8,128)} %get-tuple-element.10.key_ref), custom_call_target="tpu_custom_call" | custom-call | tf_op jit(solution)/shard_map/pick/pallas_call | solution.py:121
  89.3 0.7 broadcast_in_dim.7
  90.0 15.4 %all_to_all.22.parts_ref = f32[16,8,128]{2,1,0:T(8,128)} all-to-all(f32[16,8,128]{2,1,0:T(8,128)S(1)} %broadcast_in_dim.7), channel_id=1, replica_groups=mesh['dp'=16,'expert'=64] {'dp'}, dimensions={0} | all-to-all | bytes 131072 | tf_op jit(solution)/shard_map/all_to_all | solution.py:125
  105.4 1.8 %grads.1 = (f32[8,128]{1,0:T(8,128)}, f32[64,256]{1,0:T(8,128)}) custom-call(f32[16,8,128]{2,1,0:T(8,128)} %all_to_all.22.parts_ref, f32[8,128]{1,0:T(8,128)} %get-tuple-element.11.gating_ref, s32[8,128]{1,0:T(8,128)} %bitcast.35, bf16[128,256]{1,0:T(8,128)(2,1)} %input_ref.1), custom_call_target="tpu_custom_call" | custom-call | tf_op jit(solution)/shard_map/grads/pallas_call | solution.py:126
  107.2 1.5 %copy.14 = f32[64,1,256]{2,1,0:T(1,128)} copy(f32[64,1,256]{2,0,1:T(8,128)} %bitcast.32) | data formatting | bytes 131072 | tf_op jit(solution)/shard_map/reshape | solution.py:131
  108.7 4.6 %all-to-all-start.3 = ((f32[64,1,256]{2,1,0:T(1,128)}), f32[64,1,256]{2,1,0:T(1,128)S(1)}, u32[]{:S(2)}, u32[]{:S(2)}) async-start(f32[64,1,256]{2,1,0:T(1,128)} %copy.14), calls=%async_computation.4 | async-start | bytes 131072 | tf_op jit(solution)/shard_map/all_to_all | solution.py:131
  113.3 0.0 copy-done
  113.3 3.1 %convolution_bitcast_fusion = f32[1,256,768]{2,1,0:T(8,128)} fusion(bf16[2048,256]{1,0:T(8,128)(2,1)} %bitcast.28, bf16[2048,768]{1,0:T(8,128)(2,1)S(1)} %bitcast.26), kind=kOutput, calls=%fused_computation.2 | convolution fusion | flops 805306368 | bytes 4980736 | tf_op jit(solution)/shard_map/dot_general | solution.py:114
  116.5 8.0 %all-to-all-done.3 = f32[64,1,256]{2,1,0:T(1,128)S(1)} async-done(((f32[64,1,256]{2,1,0:T(1,128)}), f32[64,1,256]{2,1,0:T(1,128)S(1)}, u32[]{:S(2)}, u32[]{:S(2)}) %all-to-all-start.3) | async-done | bytes 65568 | tf_op jit(solution)/shard_map/all_to_all | solution.py:131
  124.5 0.7 reduce_sum.21
  125.1 13.2 %reduce-scatter.2.cloned.1.call-done = f32[2,64,768]{2,1,0:T(8,128)} async-done(((f32[32,64,768]{2,1,0:T(8,128)}), f32[2,64,768]{2,1,0:T(8,128)}) %reduce-scatter.2.cloned.1.call-update) | async-done | bytes 393232 | tf_op jit(solution)/shard_map/reduce_scatter | solution.py:110
  138.3 1.0 convert_bitcast_fusion
  139.4 0.9 copy.15
Async XLA Ops:
  7.2 106.2 %copy-start = (bf16[64,1,32,768]{3,2,1,0:T(8,128)(2,1)S(1)}, bf16[64,1,32,768]{3,2,1,0:T(8,128)(2,1)}, u32[]{:S(2)}) copy-start(bf16[64,1,32,768]{3,2,1,0:T(8,128)(2,1)} %param.11) | copy-start | bytes 9437188
  7.2 131.2 %reduce-scatter.2.cloned.1.call-start = ((), (), s32[]{:S(2)}) async-start(), calls=%async_computation.5 | async-start | bytes 6684672 | tf_op jit(solution)/shard_map/reduce_scatter | solution.py:110
  60.4 1.0 copy-start.1
  108.7 15.8 %all-to-all-start.3 = ((f32[64,1,256]{2,1,0:T(1,128)}), f32[64,1,256]{2,1,0:T(1,128)S(1)}, u32[]{:S(2)}, u32[]{:S(2)}) async-start(f32[64,1,256]{2,1,0:T(1,128)} %copy.14), calls=%async_computation.4 | async-start | bytes 131072 | tf_op jit(solution)/shard_map/all_to_all | solution.py:131
Sparse Core Ops, SparseCore 0:
  67.1 71.2 reduce-scatter.1

commit v2 on v1

--- a/solution.py
+++ b/solution.py
@@ -4,6 +4,7 @@
 from jax.experimental import pallas as pl
 from jax.experimental.pallas import tpu as pltpu
 from jax.sharding import PartitionSpec as P
+
 
 BF = jnp.bfloat16
 F32 = jnp.float32
@@ -45,6 +46,36 @@
     send_ref[...] = dot(chosen, rows_ref[...]).astype(BF)
 
 
+def turn_kernel(own, me_ref, rows_ref, mine_ref, other_ref):
+    capacity = rows_ref.shape[1]
+    turned = jnp.swapaxes(rows_ref[...].astype(F32), 0, 1)
+    first = me_ref[1] == 0
+    for chip in range(capacity // (2 * own)):
+        for j in range(own):
+            low, high = turned[2 * own * chip + j], turned[2 * own * chip + own + j]
+            mine_ref[own * chip + j] = jnp.where(first, low, high).astype(BF)
+            other_ref[own * chip + j] = jnp.where(first, high, low).astype(BF)
+
+
+def hidden_kernel(me_ref, mine_ref, theirs_ref, weight_ref, weights_ref, *out_refs):
+    chips = len(out_refs)
+    count = out_refs[0].shape[0]
+    for d, out_ref in enumerate(out_refs):
+        at = pl.ds(lax.rem(me_ref[0] + d, chips) * count, count)
+        total = dot(mine_ref[at, :], weight_ref[...]) + dot(theirs_ref[at, :], weights_ref[...])
+        out_ref[...] = total.astype(BF)
+
+
+def sum_kernel(*refs):
+    out_ref = refs[-1]
+    total = refs[0][...].astype(F32)
+    for ref in refs[1:-1]:
+        total = total + ref[...].astype(F32)
+    sources, own, _ = out_ref.shape
+    rows = [total[j * sources : (j + 1) * sources] for j in range(own)]
+    out_ref[...] = jnp.stack(rows, axis=1).astype(BF)
+
+
 def pick_kernel(back_ref, ids_ref, key_ref, out_ref):
     experts, capacity = back_ref.shape
     top, tokens = ids_ref.shape
@@ -56,7 +87,8 @@
     expert = lax.broadcasted_iota(jnp.int32, (experts, tokens), 0)
     for k in range(top):
         here = ids_ref[k : k + 1, :] == expert
-        out_ref[k : k + 1, :] = jnp.sum(jnp.where(here, dense, 0.0), axis=0, keepdims=True)
+        row = jnp.sum(jnp.where(here, dense, 0.0), axis=0, keepdims=True)
+        out_ref[:, k : k + 1, :] = jnp.broadcast_to(row[None], (out_ref.shape[0], 1, tokens))
 
 
 def grad_kernel(parts_ref, gating_ref, ids_ref, input_ref, logit_ref, term_ref):
@@ -71,7 +103,7 @@
     spread = jnp.zeros((experts, tokens), F32)
     for k in range(top):
         spread = jnp.where(ids_ref[k : k + 1, :] == expert, grad[k : k + 1, :], spread)
-    term_ref[...] = exact_dot(spread, input_ref[...].astype(F32))
+    term_ref[:, 0, :] = exact_dot(spread, input_ref[...].astype(F32))
 
 
 def whole(shape, dtype):
@@ -104,31 +136,66 @@
     outputs = saved_output.reshape(n_expert, capacity, dcols)
     hidden = saved_hidden.reshape(n_expert * capacity, ff)
     weight = down_weight.reshape(dcols, ff)
+    chips = n_dp // 2
+    own = capacity // n_dp
+    half = chips * own
+    partner = [(i, i ^ 1) for i in range(n_dp)]
+    at = lax.axis_index("dp")
+    me = jnp.stack([at // 2, at % 2])
+    weights = lax.ppermute(weight, "dp", partner)
+    got, weights = lax.optimization_barrier((got, weights))
     back = jnp.sum(got.astype(F32) * outputs.astype(F32), axis=-1)
-    by_slot = lax.optimization_barrier(jnp.swapaxes(got, 0, 1))
-    part = dot(by_slot.reshape(capacity * n_expert, dcols), weight)
-    summed = lax.psum_scatter(
-        part.reshape(capacity, n_expert, ff), "dp", scatter_dimension=0, tiled=True
-    )
-    hidden_grad = jnp.swapaxes(summed, 0, 1).astype(BF).reshape(n_expert, 1, capacity // n_dp, ff)
+    returned = lax.all_to_all(back[:, None, :], "expert", 0, 0, tiled=True)
+    step = min(16, n_expert)
+    turned = pl.BlockSpec((half, step, dcols), lambda i: (0, i, 0))
+    mine, other = pl.pallas_call(
+        lambda *refs: turn_kernel(own, *refs),
+        grid=(n_expert // step,),
+        in_specs=[
+            pl.BlockSpec(memory_space=pltpu.SMEM),
+            pl.BlockSpec((step, capacity, dcols), lambda i: (i, 0, 0)),
+        ],
+        out_specs=(turned, turned),
+        out_shape=(whole((half, n_expert, dcols), BF),) * 2,
+        name="turn",
+    )(me, got)
+    theirs = lax.ppermute(other, "dp", partner)
+    count = own * n_expert
+    in_vmem = pl.BlockSpec(memory_space=pltpu.VMEM)
+    part = pl.pallas_call(
+        hidden_kernel,
+        in_specs=[pl.BlockSpec(memory_space=pltpu.SMEM)] + [in_vmem] * 4,
+        out_shape=(whole((count, ff), BF),) * chips,
+        cost_estimate=pl.CostEstimate(
+            flops=4 * chips * count * dcols * ff,
+            bytes_accessed=4 * chips * count * ff,
+            transcendentals=0,
+        ),
+        name="hidden",
+    )(me, mine.reshape(-1, dcols), theirs.reshape(-1, dcols), weight, weights)
+    returned, part = lax.optimization_barrier((returned, part))
+    shares = [part[0]]
+    for d in range(1, chips):
+        shares.append(lax.ppermute(part[d], "dp", [(i, (i + 2 * d) % n_dp) for i in range(n_dp)]))
+    hidden_grad = pl.pallas_call(sum_kernel, out_shape=whole((n_expert, own, ff), BF), name="total")(
+        *shares
+    ).reshape(n_expert, 1, own, ff)
     down_grad = lax.dot_general(
         got.reshape(n_expert * capacity, dcols),
         hidden,
         (((0,), (0,)), ((), ())),
         preferred_element_type=F32,
     )
-    returned = lax.all_to_all(back[:, None, :], "expert", 0, 0, tiled=True)
-    picked = pl.pallas_call(pick_kernel, out_shape=whole((top, tokens), F32), name="pick")(
+    copies = pl.pallas_call(pick_kernel, out_shape=whole((n_dp, top, tokens), F32), name="pick")(
         returned.reshape(n_expert, capacity), ids, key
     )
-    copies = jnp.broadcast_to(picked, (n_dp, top, tokens))
     parts = lax.all_to_all(copies, "dp", 0, 0, tiled=True)
     logit_grad, term = pl.pallas_call(
         grad_kernel,
-        out_shape=(whole((top, tokens), F32), whole((experts, dcols), F32)),
+        out_shape=(whole((top, tokens), F32), whole((experts, 1, dcols), F32)),
         name="grads",
     )(parts, gating, ids, layer_input)
-    tiles = lax.all_to_all(term.reshape(n_expert, 1, dcols), "expert", 0, 0, tiled=True)
+    tiles = lax.all_to_all(term, "expert", 0, 0, tiled=True)
     router_grad = jnp.sum(tiles, axis=0)
     return (hidden_grad, down_grad.reshape(1, dcols, ff), logit_grad.T, router_grad)
 
@@ -143,6 +210,7 @@
         P(None, "expert", None, "dp"),
         P("expert", "dp", None),
     )
+
     return jax.shard_map(
         body,
         mesh=mesh,

time: 148 us -> 148 us (level)
  the two profiles are of different devices: /device:TPU:15 before, /device:TPU:7 now
where the time goes in v2:
time: 148 us
  starting transfers between devices  75.1 us (51%)
  waiting for transfers between devices  48.4 us (33%)
  Pallas kernels  15.7 us (11%)
  other arithmetic  3.72 us (3%)
  matrix products  3.12 us (2%)
    ppermute x7, starting transfers between devices, body(): lax.ppermute(part[d], 'dp', [(i, (i + 2 * d) % n_dp) for i in range(n_dp)])  26.2 us
    all_to_all x1, starting transfers between devices, body(): lax.all_to_all(send.reshape(n_expert, capacity, dcols), 'expert', split_a...  23.4 us
    all_to_all x1, waiting for transfers between devices, body(): lax.all_to_all(send.reshape(n_expert, capacity, dcols), 'expert', split_a...  22.9 us
    ppermute x7, waiting for transfers between devices, body(): lax.ppermute(part[d], 'dp', [(i, (i + 2 * d) % n_dp) for i in range(n_dp)])  16.8 us
    all_to_all x1, waiting for transfers between devices, body(): returned = lax.all_to_all(back[:, None, :], 'expert', 0, 0, tiled=True)  7.69 us
    all_to_all x1, starting transfers between devices, body(): parts = lax.all_to_all(copies, 'dp', 0, 0, tiled=True)  6.72 us
    all_to_all x1, starting transfers between devices, body(): returned = lax.all_to_all(back[:, None, :], 'expert', 0, 0, tiled=True)  6.21 us
    ppermute x1, starting transfers between devices, body(): theirs = lax.ppermute(other, 'dp', partner)  5.13 us
  transfers between devices with their start and end apart: 13, of which 6 were waited for; matrix products, arithmetic and copies ran while one was open for 4% of the time, Pallas kernels for 6%

profile of v2, /device:TPU:7, one launch (start us, length us, event | category | flops | bytes accessed | tf_op | source)
XLA Modules:
  0.0 147.5 jit_solution(932713045314307427)
XLA Ops:
  0.6 0.0 copy-start
  0.6 2.6 %place.1 = (bf16[2048,256]{1,0:T(8,128)(2,1)}, s32[64,128]{1,0:T(8,128)}, f32[8,128]{1,0:T(8,128)}) custom-call(s32[8,128]{1,0:T(8,128)} %bitcast.30, f32[8,128]{1,0:T(8,128)} %bitcast.33, bf16[128,256]{1,0:T(8,128)(2,1)} %refs_2_.1), custom_call_target="tpu_custom_call" | custom-call | tf_op jit(solution)/shard_map/place/pallas_call | solution.py:124
  3.2 23.4 %all-to-all-start = ((bf16[64,32,256]{2,1,0:T(8,128)(2,1)}), bf16[64,32,256]{2,1,0:T(8,128)(2,1)}, u32[]{:S(2)}, u32[]{:S(2)}) async-start(bf16[64,32,256]{2,1,0:T(8,128)(2,1)} %bitcast.27), calls=%async_computation | async-start | bytes 2097152 | tf_op jit(solution)/shard_map/all_to_all | solution.py:133
  26.6 2.9 %collective-permute-start = (bf16[256,768]{1,0:T(8,128)(2,1)}, bf16[256,768]{1,0:T(8,128)(2,1)S(1)}, u32[]{:S(2)}, u32[]{:S(2)}) collective-permute-start(bf16[256,768]{1,0:T(8,128)(2,1)} %bitcast.36), channel_id=1, source_target_pairs={{0,64},{64,0},{128,192},{192,128},{256,320},{320,256},{384,448},{4... | collective-permute-start | bytes 1179656 | tf_op jit(solution)/shard_map/ppermute | solution.py:145
  29.5 0.6 pad_add_fusion.refs_0_.me_ref
  30.1 1.0 collective-permute-done.weights_ref
  31.0 0.0 copy-start.4
  31.0 22.9 %all-to-all-done.refs_1_ = bf16[64,32,256]{2,1,0:T(8,128)(2,1)} async-done(((bf16[64,32,256]{2,1,0:T(8,128)(2,1)}), bf16[64,32,256]{2,1,0:T(8,128)(2,1)}, u32[]{:S(2)}, u32[]{:S(2)}) %all-to-all-start) | async-done | bytes 1048608 | tf_op jit(solution)/shard_map/all_to_all | solution.py:133
  53.9 3.6 %turn.1 = (bf16[16,64,256]{2,1,0:T(8,128)(2,1)}, bf16[16,64,256]{2,1,0:T(8,128)(2,1)}) custom-call(s32[2]{0:T(128)} %pad_add_fusion.refs_0_.me_ref, bf16[64,32,256]{2,1,0:T(8,128)(2,1)} %all-to-all-done.refs_1_), custom_call_target="tpu_custom_call" | custom-call | tf_op jit(solution)/shard_map/turn/pallas_call | solution.py:151
  57.6 5.1 %collective-permute-start.1 = (bf16[16,64,256]{2,1,0:T(8,128)(2,1)}, bf16[16,64,256]{2,1,0:T(8,128)(2,1)}, u32[]{:S(2)}, u32[]{:S(2)}) collective-permute-start(bf16[16,64,256]{2,1,0:T(8,128)(2,1)} %get-tuple-element.33), channel_id=1, source_target_pairs={{0,64},{64,0},{128,192},{192,128},{256,320},{320,256},{384,448},{4... | collective-permute-start | bytes 1572872 | tf_op jit(solution)/shard_map/ppermute | solution.py:162
  62.7 2.5 %fusion = f32[64,32]{1,0:T(8,128)} fusion(bf16[64,32,256]{2,1,0:T(8,128)(2,1)} %all-to-all-done.refs_1_, bf16[64,1,32,256]{3,2,1,0:T(8,128)(2,1)} %param.12), kind=kLoop, calls=%fused_computation.1 | loop fusion | flops 2095104 | bytes 2105344 | tf_op jit(solution)/shard_map/reduce_sum | solution.py:147
  65.2 0.0 copy-done.4
  65.2 6.2 %all-to-all-start.1 = ((f32[64,1,32]{2,1,0:T(1,128)}), f32[64,1,32]{2,1,0:T(1,128)S(1)}, u32[]{:S(2)}, u32[]{:S(2)}) async-start(f32[64,1,32]{2,1,0:T(1,128)} %bitcast.6), calls=%async_computation.1 | async-start | bytes 65536 | tf_op jit(solution)/shard_map/all_to_all | solution.py:148
  71.4 0.0 collective-permute-done.1
  71.5 3.2 %hidden.1 = (bf16[128,768]{1,0:T(8,128)(2,1)}, bf16[128,768]{1,0:T(8,128)(2,1)}, bf16[128,768]{1,0:T(8,128)(2,1)}, bf16[128,768]{1,0:T(8,128)(2,1)}, bf16[128,76...) custom-call(s32[2]{0:T(128)} %pad_add_fusion.refs_0_.me_ref, ...), custom_call_target="tpu_custom_call" | custom-call | flops 805306368 | bytes 3145728 | tf_op jit(solution)/shard_map/hidden/pallas_call | solution.py:165
  74.6 7.7 %all-to-all-done.1 = f32[64,1,32]{2,1,0:T(1,128)S(1)} async-done(((f32[64,1,32]{2,1,0:T(1,128)}), f32[64,1,32]{2,1,0:T(1,128)S(1)}, u32[]{:S(2)}, u32[]{:S(2)}) %all-to-all-start.1) | async-done | bytes 8224 | tf_op jit(solution)/shard_map/all_to_all | solution.py:148
  82.3 0.0 copy-start.3
  82.3 4.3 %collective-permute-start.2 = (bf16[128,768]{1,0:T(8,128)(2,1)}, bf16[128,768]{1,0:T(8,128)(2,1)S(1)}, u32[]{:S(2)}, u32[]{:S(2)}) collective-permute-start(bf16[128,768]{1,0:T(8,128)(2,1)} %get-tuple-element.44), channel_id=1, source_target_pairs={{0,128},{64,192},{128,256},{192,320},{256,384},{320,448},{384,512}... | collective-permute-start | bytes 589832 | tf_op jit(solution)/shard_map/ppermute | solution.py:179
  86.6 2.2 %collective-permute-start.3 = (bf16[128,768]{1,0:T(8,128)(2,1)}, bf16[128,768]{1,0:T(8,128)(2,1)}, u32[]{:S(2)}, u32[]{:S(2)}) collective-permute-start(bf16[128,768]{1,0:T(8,128)(2,1)} %get-tuple-element.45), channel_id=1, source_target_pairs={{0,256},{64,320},{128,384},{192,448},{256,512},{320,576},{384,640}... | collective-permute-start | bytes 589832 | tf_op jit(solution)/shard_map/ppermute | solution.py:179
  88.9 0.0 copy-done.3
  88.9 1.9 %pick.1 = f32[16,8,128]{2,1,0:T(8,128)} custom-call(f32[64,32]{1,0:T(8,128)} %bitcast.29, s32[8,128]{1,0:T(8,128)} %bitcast.31, s32[64,128]{1,0:T(8,128)} %get-tuple-element.52.key_ref), custom_call_target="tpu_custom_call" | custom-call | tf_op jit(solution)/shard_map/pick/pallas_call | solution.py:189
  90.8 6.7 %all-to-all-start.2 = ((f32[16,8,128]{2,1,0:T(8,128)}), f32[16,8,128]{2,1,0:T(8,128)S(1)}, u32[]{:S(2)}, u32[]{:S(2)}) async-start(f32[16,8,128]{2,1,0:T(8,128)} %pick.1), calls=%async_computation.2 | async-start | bytes 131072 | tf_op jit(solution)/shard_map/all_to_all | solution.py:192
  97.5 4.3 %collective-permute-start.4 = (bf16[128,768]{1,0:T(8,128)(2,1)}, bf16[128,768]{1,0:T(8,128)(2,1)}, u32[]{:S(2)}, u32[]{:S(2)}) collective-permute-start(bf16[128,768]{1,0:T(8,128)(2,1)} %get-tuple-element.46), channel_id=1, source_target_pairs={{0,384},{64,448},{128,512},{192,576},{256,640},{320,704},{384,768}... | collective-permute-start | bytes 589832 | tf_op jit(solution)/shard_map/ppermute | solution.py:179
  101.8 4.0 %collective-permute-start.5 = (bf16[128,768]{1,0:T(8,128)(2,1)}, bf16[128,768]{1,0:T(8,128)(2,1)}, u32[]{:S(2)}, u32[]{:S(2)}) collective-permute-start(bf16[128,768]{1,0:T(8,128)(2,1)} %get-tuple-element.47), channel_id=1, source_target_pairs={{0,512},{64,576},{128,640},{192,704},{256,768},{320,832},{384,896}... | collective-permute-start | bytes 589832 | tf_op jit(solution)/shard_map/ppermute | solution.py:179
  105.8 3.1 %collective-permute-start.6 = (bf16[128,768]{1,0:T(8,128)(2,1)}, bf16[128,768]{1,0:T(8,128)(2,1)}, u32[]{:S(2)}, u32[]{:S(2)}) collective-permute-start(bf16[128,768]{1,0:T(8,128)(2,1)} %get-tuple-element.48), channel_id=1, source_target_pairs={{0,640},{64,704},{128,768},{192,832},{256,896},{320,960},{384,0},{... | collective-permute-start | bytes 589832 | tf_op jit(solution)/shard_map/ppermute | solution.py:179
  108.9 0.0 all-to-all-done.2.parts_ref
  108.9 0.0 copy-start.1
  108.9 0.6 copy-done.1
  109.5 1.8 %grads.1 = (f32[8,128]{1,0:T(8,128)}, f32[64,1,256]{2,1,0:T(1,128)}) custom-call(f32[16,8,128]{2,1,0:T(8,128)} %copy-done.1, f32[8,128]{1,0:T(8,128)} %get-tuple-element.53.gating_ref, s32[8,128]{1,0:T(8,128)} %bitcast.32, bf16[128,256]{1,0:T(8,128)(2,1)} %input_ref.1), custom_call_target="tpu_custom_call" | custom-call | tf_op jit(solution)/shard_map/grads/pallas_call | solution.py:193
  111.3 4.6 %all-to-all-start.3 = ((f32[64,1,256]{2,1,0:T(1,128)}), f32[64,1,256]{2,1,0:T(1,128)S(1)}, u32[]{:S(2)}, u32[]{:S(2)}) async-start(f32[64,1,256]{2,1,0:T(1,128)} %get-tuple-element.55), calls=%async_computation.3 | async-start | bytes 131072 | tf_op jit(solution)/shard_map/all_to_all | solution.py:198
  115.9 0.0 collective-permute-done.2.refs_1_
  115.9 0.0 copy-start.2
  115.9 5.2 %collective-permute-start.7 = (bf16[128,768]{1,0:T(8,128)(2,1)}, bf16[128,768]{1,0:T(8,128)(2,1)}, u32[]{:S(2)}, u32[]{:S(2)}) collective-permute-start(bf16[128,768]{1,0:T(8,128)(2,1)} %get-tuple-element.49), channel_id=1, source_target_pairs={{0,768},{64,832},{128,896},{192,960},{256,0},{320,64},{384,128},{4... | collective-permute-start | bytes 589832 | tf_op jit(solution)/shard_map/ppermute | solution.py:179
  121.1 0.0 collective-permute-done.3.refs_2_
  121.1 3.1 %collective-permute-start.8 = (bf16[128,768]{1,0:T(8,128)(2,1)}, bf16[128,768]{1,0:T(8,128)(2,1)}, u32[]{:S(2)}, u32[]{:S(2)}) collective-permute-start(bf16[128,768]{1,0:T(8,128)(2,1)} %get-tuple-element.50), channel_id=1, source_target_pairs={{0,896},{64,960},{128,0},{192,64},{256,128},{320,192},{384,256},{4... | collective-permute-start | bytes 589832 | tf_op jit(solution)/shard_map/ppermute | solution.py:179
  124.2 0.0 copy-done
  124.3 3.1 %convolution_bitcast_fusion = f32[1,256,768]{2,1,0:T(8,128)} fusion(bf16[2048,256]{1,0:T(8,128)(2,1)} %bitcast.13, bf16[2048,768]{1,0:T(8,128)(2,1)S(1)} %bitcast.26), kind=kOutput, calls=%fused_computation.2 | convolution fusion | flops 805306368 | bytes 4980736 | tf_op jit(solution)/shard_map/dot_general | solution.py:183
  127.4 0.0 collective-permute-done.4.refs_3_
  127.4 0.0 collective-permute-done.5.refs_4_
  127.4 3.9 %collective-permute-done.6.refs_5_ = bf16[128,768]{1,0:T(8,128)(2,1)} collective-permute-done((bf16[128,768]{1,0:T(8,128)(2,1)}, bf16[128,768]{1,0:T(8,128)(2,1)}, u32[]{:S(2)}, u32[]{:S(2)}) %collective-permute-start.6) | collective-permute-done | bytes 196640 | tf_op jit(solution)/shard_map/ppermute | solution.py:179
  131.3 4.1 %collective-permute-done.7.refs_6_ = bf16[128,768]{1,0:T(8,128)(2,1)} collective-permute-done((bf16[128,768]{1,0:T(8,128)(2,1)}, bf16[128,768]{1,0:T(8,128)(2,1)}, u32[]{:S(2)}, u32[]{:S(2)}) %collective-permute-start.7) | collective-permute-done | bytes 196640 | tf_op jit(solution)/shard_map/ppermute | solution.py:179
  135.4 8.8 %collective-permute-done.8.refs_7_ = bf16[128,768]{1,0:T(8,128)(2,1)} collective-permute-done((bf16[128,768]{1,0:T(8,128)(2,1)}, bf16[128,768]{1,0:T(8,128)(2,1)}, u32[]{:S(2)}, u32[]{:S(2)}) %collective-permute-start.8) | collective-permute-done | bytes 196640 | tf_op jit(solution)/shard_map/ppermute | solution.py:179
  144.2 0.0 copy-done.2
  144.2 2.6 %total.1 = bf16[64,2,768]{2,1,0:T(2,128)(2,1)} custom-call(bf16[128,768]{1,0:T(8,128)(2,1)} %get-tuple-element.43.refs_0_, bf16[128,768]{1,0:T(8,128)(2,1)} %copy-done.2, bf16[128,768]{1,0:T(8,128)(2,1)} %collective-permute-done.3.refs_2_, bf16[128,768]{1,0:T(8,128)(2,1)} %collective-permute-done.4.refs_3_, bf16[128,768]{1,0:T(8,128)(2,1)} %collective-permute-done.5.refs_4_, ...), custom_call_target="tpu_custom_call" | custom-call | tf_op jit(solution)/shard_map/total/pallas_call | solution.py:180
  146.9 0.0 all-to-all-done.3
  146.9 0.7 reduce_sum.21
Async XLA Ops:
  0.6 123.6 %copy-start = (bf16[64,1,32,768]{3,2,1,0:T(8,128)(2,1)S(1)}, bf16[64,1,32,768]{3,2,1,0:T(8,128)(2,1)}, u32[]{:S(2)}) copy-start(bf16[64,1,32,768]{3,2,1,0:T(8,128)(2,1)} %param.11) | copy-start | bytes 9437188
  3.2 50.7 %all-to-all-start = ((bf16[64,32,256]{2,1,0:T(8,128)(2,1)}), bf16[64,32,256]{2,1,0:T(8,128)(2,1)}, u32[]{:S(2)}, u32[]{:S(2)}) async-start(bf16[64,32,256]{2,1,0:T(8,128)(2,1)} %bitcast.27), calls=%async_computation | async-start | bytes 2097152 | tf_op jit(solution)/shard_map/all_to_all | solution.py:133
  26.6 4.4 %collective-permute-start = (bf16[256,768]{1,0:T(8,128)(2,1)}, bf16[256,768]{1,0:T(8,128)(2,1)S(1)}, u32[]{:S(2)}, u32[]{:S(2)}) collective-permute-start(bf16[256,768]{1,0:T(8,128)(2,1)} %bitcast.36), channel_id=1, source_target_pairs={{0,64},{64,0},{128,192},{192,128},{256,320},{320,256},{384,448},{4... | collective-permute-start | bytes 1179656 | tf_op jit(solution)/shard_map/ppermute | solution.py:145
  31.0 34.2 %copy-start.4 = (bf16[256,768]{1,0:T(8,128)(2,1)}, bf16[256,768]{1,0:T(8,128)(2,1)S(1)}, u32[]{:S(2)}) copy-start(bf16[256,768]{1,0:T(8,128)(2,1)S(1)} %collective-permute-done.weights_ref) | copy-start | bytes 1179652
  57.6 13.9 %collective-permute-start.1 = (bf16[16,64,256]{2,1,0:T(8,128)(2,1)}, bf16[16,64,256]{2,1,0:T(8,128)(2,1)}, u32[]{:S(2)}, u32[]{:S(2)}) collective-permute-start(bf16[16,64,256]{2,1,0:T(8,128)(2,1)} %get-tuple-element.33), channel_id=1, source_target_pairs={{0,64},{64,0},{128,192},{192,128},{256,320},{320,256},{384,448},{4... | collective-permute-start | bytes 1572872 | tf_op jit(solution)/shard_map/ppermute | solution.py:162
  65.2 17.1 %all-to-all-start.1 = ((f32[64,1,32]{2,1,0:T(1,128)}), f32[64,1,32]{2,1,0:T(1,128)S(1)}, u32[]{:S(2)}, u32[]{:S(2)}) async-start(f32[64,1,32]{2,1,0:T(1,128)} %bitcast.6), calls=%async_computation.1 | async-start | bytes 65536 | tf_op jit(solution)/shard_map/all_to_all | solution.py:148
  82.3 6.6 %copy-start.3 = (f32[64,1,32]{2,1,0:T(1,128)}, f32[64,1,32]{2,1,0:T(1,128)S(1)}, u32[]{:S(2)}) copy-start(f32[64,1,32]{2,1,0:T(1,128)S(1)} %all-to-all-done.1) | copy-start | bytes 24580
  82.3 33.6 %collective-permute-start.2 = (bf16[128,768]{1,0:T(8,128)(2,1)}, bf16[128,768]{1,0:T(8,128)(2,1)S(1)}, u32[]{:S(2)}, u32[]{:S(2)}) collective-permute-start(bf16[128,768]{1,0:T(8,128)(2,1)} %get-tuple-element.44), channel_id=1, source_target_pairs={{0,128},{64,192},{128,256},{192,320},{256,384},{320,448},{384,512}... | collective-permute-start | bytes 589832 | tf_op jit(solution)/shard_map/ppermute | solution.py:179
  86.6 34.5 %collective-permute-start.3 = (bf16[128,768]{1,0:T(8,128)(2,1)}, bf16[128,768]{1,0:T(8,128)(2,1)}, u32[]{:S(2)}, u32[]{:S(2)}) collective-permute-start(bf16[128,768]{1,0:T(8,128)(2,1)} %get-tuple-element.45), channel_id=1, source_target_pairs={{0,256},{64,320},{128,384},{192,448},{256,512},{320,576},{384,640}... | collective-permute-start | bytes 589832 | tf_op jit(solution)/shard_map/ppermute | solution.py:179
  90.8 18.1 %all-to-all-start.2 = ((f32[16,8,128]{2,1,0:T(8,128)}), f32[16,8,128]{2,1,0:T(8,128)S(1)}, u32[]{:S(2)}, u32[]{:S(2)}) async-start(f32[16,8,128]{2,1,0:T(8,128)} %pick.1), calls=%async_computation.2 | async-start | bytes 131072 | tf_op jit(solution)/shard_map/all_to_all | solution.py:192
  97.5 29.9 %collective-permute-start.4 = (bf16[128,768]{1,0:T(8,128)(2,1)}, bf16[128,768]{1,0:T(8,128)(2,1)}, u32[]{:S(2)}, u32[]{:S(2)}) collective-permute-start(bf16[128,768]{1,0:T(8,128)(2,1)} %get-tuple-element.46), channel_id=1, source_target_pairs={{0,384},{64,448},{128,512},{192,576},{256,640},{320,704},{384,768}... | collective-permute-start | bytes 589832 | tf_op jit(solution)/shard_map/ppermute | solution.py:179
  101.8 25.6 %collective-permute-start.5 = (bf16[128,768]{1,0:T(8,128)(2,1)}, bf16[128,768]{1,0:T(8,128)(2,1)}, u32[]{:S(2)}, u32[]{:S(2)}) collective-permute-start(bf16[128,768]{1,0:T(8,128)(2,1)} %get-tuple-element.47), channel_id=1, source_target_pairs={{0,512},{64,576},{128,640},{192,704},{256,768},{320,832},{384,896}... | collective-permute-start | bytes 589832 | tf_op jit(solution)/shard_map/ppermute | solution.py:179
  105.8 25.5 %collective-permute-start.6 = (bf16[128,768]{1,0:T(8,128)(2,1)}, bf16[128,768]{1,0:T(8,128)(2,1)}, u32[]{:S(2)}, u32[]{:S(2)}) collective-permute-start(bf16[128,768]{1,0:T(8,128)(2,1)} %get-tuple-element.48), channel_id=1, source_target_pairs={{0,640},{64,704},{128,768},{192,832},{256,896},{320,960},{384,0},{... | collective-permute-start | bytes 589832 | tf_op jit(solution)/shard_map/ppermute | solution.py:179
  108.9 0.6 copy-start.1
  111.3 35.6 %all-to-all-start.3 = ((f32[64,1,256]{2,1,0:T(1,128)}), f32[64,1,256]{2,1,0:T(1,128)S(1)}, u32[]{:S(2)}, u32[]{:S(2)}) async-start(f32[64,1,256]{2,1,0:T(1,128)} %get-tuple-element.55), calls=%async_computation.3 | async-start | bytes 131072 | tf_op jit(solution)/shard_map/all_to_all | solution.py:198
  115.9 28.3 %copy-start.2 = (bf16[128,768]{1,0:T(8,128)(2,1)}, bf16[128,768]{1,0:T(8,128)(2,1)S(1)}, u32[]{:S(2)}) copy-start(bf16[128,768]{1,0:T(8,128)(2,1)S(1)} %collective-permute-done.2.refs_1_) | copy-start | bytes 589828
  115.9 19.5 %collective-permute-start.7 = (bf16[128,768]{1,0:T(8,128)(2,1)}, bf16[128,768]{1,0:T(8,128)(2,1)}, u32[]{:S(2)}, u32[]{:S(2)}) collective-permute-start(bf16[128,768]{1,0:T(8,128)(2,1)} %get-tuple-element.49), channel_id=1, source_target_pairs={{0,768},{64,832},{128,896},{192,960},{256,0},{320,64},{384,128},{4... | collective-permute-start | bytes 589832 | tf_op jit(solution)/shard_map/ppermute | solution.py:179
  121.1 23.1 %collective-permute-start.8 = (bf16[128,768]{1,0:T(8,128)(2,1)}, bf16[128,768]{1,0:T(8,128)(2,1)}, u32[]{:S(2)}, u32[]{:S(2)}) collective-permute-start(bf16[128,768]{1,0:T(8,128)(2,1)} %get-tuple-element.50), channel_id=1, source_target_pairs={{0,896},{64,960},{128,0},{192,64},{256,128},{320,192},{384,256},{4... | collective-permute-start | bytes 589832 | tf_op jit(solution)/shard_map/ppermute | solution.py:179

commit v3 on v2

--- a/solution.py
+++ b/solution.py
@@ -46,24 +46,29 @@
     send_ref[...] = dot(chosen, rows_ref[...]).astype(BF)
 
 
-def turn_kernel(own, me_ref, rows_ref, mine_ref, other_ref):
-    capacity = rows_ref.shape[1]
-    turned = jnp.swapaxes(rows_ref[...].astype(F32), 0, 1)
-    first = me_ref[1] == 0
-    for chip in range(capacity // (2 * own)):
-        for j in range(own):
-            low, high = turned[2 * own * chip + j], turned[2 * own * chip + own + j]
-            mine_ref[own * chip + j] = jnp.where(first, low, high).astype(BF)
-            other_ref[own * chip + j] = jnp.where(first, high, low).astype(BF)
-
-
-def hidden_kernel(me_ref, mine_ref, theirs_ref, weight_ref, weights_ref, *out_refs):
-    chips = len(out_refs)
+def turn_kernel(own, me_ref, rows_ref, *refs):
+    *out_refs, turned_ref = refs
+    members = len(out_refs)
+    turned_ref[...] = jnp.swapaxes(rows_ref[...].astype(F32), 0, 1).astype(BF)
+    for p, out_ref in enumerate(out_refs):
+        member = jnp.bitwise_xor(me_ref[1], p)
+        for at in range(out_ref.shape[0]):
+            base = (at // own) * members * own + at % own
+            out_ref[at] = turned_ref[base + member * own]
+
+
+def hidden_kernel(members, me_ref, *refs):
+    rows_refs, weight_refs = refs[:members], refs[members : 2 * members]
+    *out_refs, total_ref = refs[2 * members :]
+    total = dot(rows_refs[0][...], weight_refs[0][...])
+    for rows_ref, weight_ref in zip(rows_refs[1:], weight_refs[1:]):
+        total = total + dot(rows_ref[...], weight_ref[...])
+    total_ref[...] = total
+    groups = len(out_refs)
     count = out_refs[0].shape[0]
     for d, out_ref in enumerate(out_refs):
-        at = pl.ds(lax.rem(me_ref[0] + d, chips) * count, count)
-        total = dot(mine_ref[at, :], weight_ref[...]) + dot(theirs_ref[at, :], weights_ref[...])
-        out_ref[...] = total.astype(BF)
+        at = pl.ds(pl.multiple_of(lax.rem(me_ref[0] + d, groups) * count, count), count)
+        out_ref[...] = total_ref[at, :].astype(BF)
 
 
 def sum_kernel(*refs):
@@ -136,47 +141,54 @@
     outputs = saved_output.reshape(n_expert, capacity, dcols)
     hidden = saved_hidden.reshape(n_expert * capacity, ff)
     weight = down_weight.reshape(dcols, ff)
-    chips = n_dp // 2
+    members = 4
+    groups = n_dp // members
     own = capacity // n_dp
-    half = chips * own
-    partner = [(i, i ^ 1) for i in range(n_dp)]
+    mine = groups * own
     at = lax.axis_index("dp")
-    me = jnp.stack([at // 2, at % 2])
-    weights = lax.ppermute(weight, "dp", partner)
+    me = jnp.stack([lax.div(at, members), lax.rem(at, members)])
+
+    def swapped(x, p):
+        return lax.ppermute(x, "dp", [(i, i ^ p) for i in range(n_dp)])
+
+    weights = [weight] + [swapped(weight, p) for p in range(1, members)]
     got, weights = lax.optimization_barrier((got, weights))
     back = jnp.sum(got.astype(F32) * outputs.astype(F32), axis=-1)
     returned = lax.all_to_all(back[:, None, :], "expert", 0, 0, tiled=True)
     step = min(16, n_expert)
-    turned = pl.BlockSpec((half, step, dcols), lambda i: (0, i, 0))
-    mine, other = pl.pallas_call(
+    turned = pl.BlockSpec((mine, step, dcols), lambda i: (0, i, 0))
+    sets = pl.pallas_call(
         lambda *refs: turn_kernel(own, *refs),
         grid=(n_expert // step,),
         in_specs=[
             pl.BlockSpec(memory_space=pltpu.SMEM),
             pl.BlockSpec((step, capacity, dcols), lambda i: (i, 0, 0)),
         ],
-        out_specs=(turned, turned),
-        out_shape=(whole((half, n_expert, dcols), BF),) * 2,
+        out_specs=(turned,) * members,
+        out_shape=(whole((mine, n_expert, dcols), BF),) * members,
+        scratch_shapes=[pltpu.VMEM((capacity, step, dcols), BF)],
         name="turn",
     )(me, got)
-    theirs = lax.ppermute(other, "dp", partner)
+    rows = [sets[0]] + [swapped(sets[p], p) for p in range(1, members)]
     count = own * n_expert
     in_vmem = pl.BlockSpec(memory_space=pltpu.VMEM)
     part = pl.pallas_call(
-        hidden_kernel,
-        in_specs=[pl.BlockSpec(memory_space=pltpu.SMEM)] + [in_vmem] * 4,
-        out_shape=(whole((count, ff), BF),) * chips,
+        lambda *refs: hidden_kernel(members, *refs),
+        in_specs=[pl.BlockSpec(memory_space=pltpu.SMEM)] + [in_vmem] * (2 * members),
+        out_shape=(whole((count, ff), BF),) * groups,
+        scratch_shapes=[pltpu.VMEM((groups * count, ff), F32)],
         cost_estimate=pl.CostEstimate(
-            flops=4 * chips * count * dcols * ff,
-            bytes_accessed=4 * chips * count * ff,
+            flops=2 * members * groups * count * dcols * ff,
+            bytes_accessed=4 * groups * count * ff,
             transcendentals=0,
         ),
         name="hidden",
-    )(me, mine.reshape(-1, dcols), theirs.reshape(-1, dcols), weight, weights)
-    returned, part = lax.optimization_barrier((returned, part))
+    )(me, *[r.reshape(-1, dcols) for r in rows], *weights)
     shares = [part[0]]
-    for d in range(1, chips):
-        shares.append(lax.ppermute(part[d], "dp", [(i, (i + 2 * d) % n_dp) for i in range(n_dp)]))
+    for d in range(1, groups):
+        shares.append(
+            lax.ppermute(part[d], "dp", [(i, (i + members * d) % n_dp) for i in range(n_dp)])
+        )
     hidden_grad = pl.pallas_call(sum_kernel, out_shape=whole((n_expert, own, ff), BF), name="total")(
         *shares
     ).reshape(n_expert, 1, own, ff)

time: 148 us -> 147 us (level)
  the two profiles are of different devices: /device:TPU:7 before, /device:TPU:1 now
where the time goes in v3:
time: 147 us; the launch traced here: 146 us
  starting transfers between devices  57.5 us (39%)
  blocking collectives  33.3 us (23%)
  waiting for transfers between devices  32.5 us (22%)
  Pallas kernels  15.9 us (11%)
  other arithmetic  3.2 us (2%)
  matrix products  3.12 us (2%)
    all_to_all x1, starting transfers between devices, body(): lax.all_to_all(send.reshape(n_expert, capacity, dcols), 'expert', split_a...  24.2 us
    ppermute x6, starting transfers between devices, swapped(): return lax.ppermute(x, 'dp', [(i, i ^ p) for i in range(n_dp)])  18.8 us
    all_to_all x1, blocking collectives, body(): returned = lax.all_to_all(back[:, None, :], 'expert', 0, 0, tiled=True)  16.9 us
    all_to_all x1, blocking collectives, body(): parts = lax.all_to_all(copies, 'dp', 0, 0, tiled=True)  16.4 us
    ppermute x3, waiting for transfers between devices, body(): lax.ppermute(part[d], 'dp', [(i, (i + members * d) % n_dp) for i in range...  14.1 us
    ppermute x6, waiting for transfers between devices, swapped(): return lax.ppermute(x, 'dp', [(i, i ^ p) for i in range(n_dp)])  13.7 us
    ppermute x3, starting transfers between devices, body(): lax.ppermute(part[d], 'dp', [(i, (i + members * d) % n_dp) for i in range...  9.87 us
    all_to_all x1, waiting for transfers between devices, body(): lax.all_to_all(send.reshape(n_expert, capacity, dcols), 'expert', split_a...  4.76 us
  transfers between devices with their start and end apart: 11, of which 6 were waited for; matrix products, arithmetic and copies ran while one was open for 4% of the time, Pallas kernels for 5%

profile of v3, /device:TPU:1, one launch (start us, length us, event | category | flops | bytes accessed | tf_op | source)
XLA Modules:
  0.0 146.4 jit_solution(7430411294744558503)
XLA Ops:
  0.6 0.0 copy-start
  0.6 2.6 %place.1 = (bf16[2048,256]{1,0:T(8,128)(2,1)}, s32[64,128]{1,0:T(8,128)}, f32[8,128]{1,0:T(8,128)}) custom-call(s32[8,128]{1,0:T(8,128)} %bitcast.33, f32[8,128]{1,0:T(8,128)} %bitcast.36, bf16[128,256]{1,0:T(8,128)(2,1)} %refs_2_.1), custom_call_target="tpu_custom_call" | custom-call | tf_op jit(solution)/shard_map/place/pallas_call | solution.py:129
  3.2 24.2 %all-to-all-start = ((bf16[64,32,256]{2,1,0:T(8,128)(2,1)}), bf16[64,32,256]{2,1,0:T(8,128)(2,1)}, u32[]{:S(2)}, u32[]{:S(2)}) async-start(bf16[64,32,256]{2,1,0:T(8,128)(2,1)} %bitcast.29), calls=%async_computation | async-start | bytes 2097152 | tf_op jit(solution)/shard_map/all_to_all | solution.py:138
  27.5 4.0 %collective-permute-start.2 = (bf16[256,768]{1,0:T(8,128)(2,1)}, bf16[256,768]{1,0:T(8,128)(2,1)S(1)}, u32[]{:S(2)}, u32[]{:S(2)}) collective-permute-start(bf16[256,768]{1,0:T(8,128)(2,1)} %bitcast.38), channel_id=1, source_target_pairs={{0,192},{64,128},{128,64},{192,0},{256,448},{320,384},{384,320},{4... | collective-permute-start | bytes 1179656 | tf_op jit(solution)/shard_map/ppermute | solution.py:152
  31.4 2.2 %collective-permute-start.1 = (bf16[256,768]{1,0:T(8,128)(2,1)}, bf16[256,768]{1,0:T(8,128)(2,1)}, u32[]{:S(2)}, u32[]{:S(2)}) collective-permute-start(bf16[256,768]{1,0:T(8,128)(2,1)} %bitcast.39), channel_id=1, source_target_pairs={{0,128},{64,192},{128,0},{192,64},{256,384},{320,448},{384,256},{4... | collective-permute-start | bytes 1179656 | tf_op jit(solution)/shard_map/ppermute | solution.py:152
  33.6 2.1 %collective-permute-start = (bf16[256,768]{1,0:T(8,128)(2,1)}, bf16[256,768]{1,0:T(8,128)(2,1)}, u32[]{:S(2)}, u32[]{:S(2)}) collective-permute-start(bf16[256,768]{1,0:T(8,128)(2,1)} %bitcast.40), channel_id=1, source_target_pairs={{0,64},{64,0},{128,192},{192,128},{256,320},{320,256},{384,448},{4... | collective-permute-start | bytes 1179656 | tf_op jit(solution)/shard_map/ppermute | solution.py:152
  35.7 0.6 pad_add_fusion.refs_0_
  36.3 5.4 %collective-permute-done.2.refs_8_ = bf16[256,768]{1,0:T(8,128)(2,1)S(1)} collective-permute-done((bf16[256,768]{1,0:T(8,128)(2,1)}, bf16[256,768]{1,0:T(8,128)(2,1)S(1)}, u32[]{:S(2)}, u32[]{:S(2)}) %collective-permute-start.2) | collective-permute-done | bytes 393248 | tf_op jit(solution)/shard_map/ppermute | solution.py:152
  41.7 0.0 copy-start.2
  41.7 8.3 %collective-permute-done.1.refs_7_ = bf16[256,768]{1,0:T(8,128)(2,1)} collective-permute-done((bf16[256,768]{1,0:T(8,128)(2,1)}, bf16[256,768]{1,0:T(8,128)(2,1)}, u32[]{:S(2)}, u32[]{:S(2)}) %collective-permute-start.1) | collective-permute-done | bytes 393248 | tf_op jit(solution)/shard_map/ppermute | solution.py:152
  50.0 0.0 collective-permute-done.refs_6_
  50.0 4.8 %all-to-all-done.refs_1_ = bf16[64,32,256]{2,1,0:T(8,128)(2,1)} async-done(((bf16[64,32,256]{2,1,0:T(8,128)(2,1)}), bf16[64,32,256]{2,1,0:T(8,128)(2,1)}, u32[]{:S(2)}, u32[]{:S(2)}) %all-to-all-start) | async-done | bytes 1048608 | tf_op jit(solution)/shard_map/all_to_all | solution.py:138
  54.8 3.7 %turn.1 = (bf16[8,64,256]{2,1,0:T(8,128)(2,1)}, bf16[8,64,256]{2,1,0:T(8,128)(2,1)}, bf16[8,64,256]{2,1,0:T(8,128)(2,1)}, bf16[8,64,256]{2,1,0:T(8,128)(2,1)}) custom-call(s32[2]{0:T(128)} %pad_add_fusion.refs_0_, bf16[64,32,256]{2,1,0:T(8,128)(2,1)} %all-to-all-done.refs_1_), custom_call_target="tpu_custom_call" | custom-call | tf_op jit(solution)/shard_map/turn/pallas_call | solution.py:160
  58.5 5.1 %collective-permute-start.3 = (bf16[8,64,256]{2,1,0:T(8,128)(2,1)}, bf16[8,64,256]{2,1,0:T(8,128)(2,1)}, u32[]{:S(2)}, u32[]{:S(2)}) collective-permute-start(bf16[8,64,256]{2,1,0:T(8,128)(2,1)} %get-tuple-element.25), channel_id=1, source_target_pairs={{0,64},{64,0},{128,192},{192,128},{256,320},{320,256},{384,448},{4... | collective-permute-start | bytes 786440 | tf_op jit(solution)/shard_map/ppermute | solution.py:152
  63.6 3.1 %collective-permute-start.4 = (bf16[8,64,256]{2,1,0:T(8,128)(2,1)}, bf16[8,64,256]{2,1,0:T(8,128)(2,1)}, u32[]{:S(2)}, u32[]{:S(2)}) collective-permute-start(bf16[8,64,256]{2,1,0:T(8,128)(2,1)} %get-tuple-element.26), channel_id=1, source_target_pairs={{0,128},{64,192},{128,0},{192,64},{256,384},{320,448},{384,256},{4... | collective-permute-start | bytes 786440 | tf_op jit(solution)/shard_map/ppermute | solution.py:152
  66.8 2.3 %collective-permute-start.5 = (bf16[8,64,256]{2,1,0:T(8,128)(2,1)}, bf16[8,64,256]{2,1,0:T(8,128)(2,1)}, u32[]{:S(2)}, u32[]{:S(2)}) collective-permute-start(bf16[8,64,256]{2,1,0:T(8,128)(2,1)} %get-tuple-element.27), channel_id=1, source_target_pairs={{0,192},{64,128},{128,64},{192,0},{256,448},{320,384},{384,320},{4... | collective-permute-start | bytes 786440 | tf_op jit(solution)/shard_map/ppermute | solution.py:152
  69.1 1.9 %fusion = f32[64,32]{1,0:T(8,128)S(1)} fusion(bf16[64,32,256]{2,1,0:T(8,128)(2,1)} %all-to-all-done.refs_1_, bf16[64,1,32,256]{3,2,1,0:T(8,128)(2,1)} %param.12), kind=kLoop, calls=%fused_computation.1 | loop fusion | flops 2095104 | bytes 2105344 | tf_op jit(solution)/shard_map/reduce_sum | solution.py:156
  71.0 16.9 %all_to_all.20 = f32[64,1,32]{2,1,0:T(1,128)} all-to-all(f32[64,1,32]{2,1,0:T(1,128)S(1)} %bitcast.31), channel_id=1, replica_groups=mesh['dp'=16,'expert'=64] {'expert'}, dimensions={0} | all-to-all | bytes 16384 | tf_op jit(solution)/shard_map/all_to_all | solution.py:157
  87.9 1.9 %pick.1 = f32[16,8,128]{2,1,0:T(8,128)} custom-call(f32[64,32]{1,0:T(8,128)} %bitcast.32, s32[8,128]{1,0:T(8,128)} %bitcast.34, s32[64,128]{1,0:T(8,128)} %get-tuple-element.36.key_ref), custom_call_target="tpu_custom_call" | custom-call | tf_op jit(solution)/shard_map/pick/pallas_call | solution.py:201
  89.8 16.4 %all_to_all.21.parts_ref = f32[16,8,128]{2,1,0:T(8,128)} all-to-all(f32[16,8,128]{2,1,0:T(8,128)} %pick.1), channel_id=1, replica_groups=mesh['dp'=16,'expert'=64] {'dp'}, dimensions={0} | all-to-all | bytes 131072 | tf_op jit(solution)/shard_map/all_to_all | solution.py:204
  106.2 1.8 %grads.1 = (f32[8,128]{1,0:T(8,128)}, f32[64,1,256]{2,1,0:T(1,128)}) custom-call(f32[16,8,128]{2,1,0:T(8,128)} %all_to_all.21.parts_ref, f32[8,128]{1,0:T(8,128)} %get-tuple-element.37.gating_ref, s32[8,128]{1,0:T(8,128)} %bitcast.35, bf16[128,256]{1,0:T(8,128)(2,1)} %input_ref.1), custom_call_target="tpu_custom_call" | custom-call | tf_op jit(solution)/shard_map/grads/pallas_call | solution.py:205
  108.0 0.0 copy-done.2
  108.0 4.6 %all-to-all-start.3 = ((f32[64,1,256]{2,1,0:T(1,128)}), f32[64,1,256]{2,1,0:T(1,128)S(1)}, u32[]{:S(2)}, u32[]{:S(2)}) async-start(f32[64,1,256]{2,1,0:T(1,128)} %get-tuple-element.39), calls=%async_computation.3 | async-start | bytes 131072 | tf_op jit(solution)/shard_map/all_to_all | solution.py:210
  112.6 0.0 collective-permute-done.3
  112.6 0.0 collective-permute-done.4
  112.6 0.0 collective-permute-done.5
  112.6 3.7 %hidden.1 = (bf16[128,768]{1,0:T(8,128)(2,1)}, bf16[128,768]{1,0:T(8,128)(2,1)}, bf16[128,768]{1,0:T(8,128)(2,1)}, bf16[128,768]{1,0:T(8,128)(2,1)}) custom-call(s32[2]{0:T(128)} %pad_add_fusion.refs_0_, bf16[512,256]{1,0:T(8,128)(2,1)} %bitcast.42, bf16[512,256]{1,0:T(8,128)(2,1)} %bitcast.7.refs_2_, bf16[512,256]{1,0:T(8,128)(2,1)} %bitcast.8.refs_3_, ...), custom_call_target="tpu_custom_call" | custom-call | flops 805306368 | bytes 1572864 | tf_op jit(solution)/shard_map/hidden/pallas_call | solution.py:175
  116.3 2.1 %collective-permute-start.6 = (bf16[128,768]{1,0:T(8,128)(2,1)}, bf16[128,768]{1,0:T(8,128)(2,1)S(1)}, u32[]{:S(2)}, u32[]{:S(2)}) collective-permute-start(bf16[128,768]{1,0:T(8,128)(2,1)} %get-tuple-element.33), channel_id=1, source_target_pairs={{0,256},{64,320},{128,384},{192,448},{256,512},{320,576},{384,640}... | collective-permute-start | bytes 589832 | tf_op jit(solution)/shard_map/ppermute | solution.py:190
  118.5 4.0 %collective-permute-start.7 = (bf16[128,768]{1,0:T(8,128)(2,1)}, bf16[128,768]{1,0:T(8,128)(2,1)}, u32[]{:S(2)}, u32[]{:S(2)}) collective-permute-start(bf16[128,768]{1,0:T(8,128)(2,1)} %get-tuple-element.34), channel_id=1, source_target_pairs={{0,512},{64,576},{128,640},{192,704},{256,768},{320,832},{384,896}... | collective-permute-start | bytes 589832 | tf_op jit(solution)/shard_map/ppermute | solution.py:190
  122.5 3.7 %collective-permute-start.8 = (bf16[128,768]{1,0:T(8,128)(2,1)}, bf16[128,768]{1,0:T(8,128)(2,1)}, u32[]{:S(2)}, u32[]{:S(2)}) collective-permute-start(bf16[128,768]{1,0:T(8,128)(2,1)} %get-tuple-element.35), channel_id=1, source_target_pairs={{0,768},{64,832},{128,896},{192,960},{256,0},{320,64},{384,128},{4... | collective-permute-start | bytes 589832 | tf_op jit(solution)/shard_map/ppermute | solution.py:190
  126.2 0.0 copy-done
  126.2 3.1 %convolution_bitcast_fusion = f32[1,256,768]{2,1,0:T(8,128)} fusion(bf16[2048,256]{1,0:T(8,128)(2,1)} %bitcast.12, bf16[2048,768]{1,0:T(8,128)(2,1)S(1)} %bitcast.28), kind=kOutput, calls=%fused_computation.2 | convolution fusion | flops 805306368 | bytes 4980736 | tf_op jit(solution)/shard_map/dot_general | solution.py:195
  129.3 0.0 all-to-all-done.3
  129.3 0.7 reduce_sum.21
  130.0 3.6 %collective-permute-done.6.refs_1_ = bf16[128,768]{1,0:T(8,128)(2,1)S(1)} collective-permute-done((bf16[128,768]{1,0:T(8,128)(2,1)}, bf16[128,768]{1,0:T(8,128)(2,1)S(1)}, u32[]{:S(2)}, u32[]{:S(2)}) %collective-permute-start.6) | collective-permute-done | bytes 196640 | tf_op jit(solution)/shard_map/ppermute | solution.py:190
  133.6 0.0 copy-start.1
  133.6 2.3 %collective-permute-done.7.refs_2_ = bf16[128,768]{1,0:T(8,128)(2,1)} collective-permute-done((bf16[128,768]{1,0:T(8,128)(2,1)}, bf16[128,768]{1,0:T(8,128)(2,1)}, u32[]{:S(2)}, u32[]{:S(2)}) %collective-permute-start.7) | collective-permute-done | bytes 196640 | tf_op jit(solution)/shard_map/ppermute | solution.py:190
  135.9 8.2 %collective-permute-done.8.refs_3_ = bf16[128,768]{1,0:T(8,128)(2,1)} collective-permute-done((bf16[128,768]{1,0:T(8,128)(2,1)}, bf16[128,768]{1,0:T(8,128)(2,1)}, u32[]{:S(2)}, u32[]{:S(2)}) %collective-permute-start.8) | collective-permute-done | bytes 196640 | tf_op jit(solution)/shard_map/ppermute | solution.py:190
  144.1 0.0 copy-done.1
  144.1 2.3 %total.1 = bf16[64,2,768]{2,1,0:T(2,128)(2,1)} custom-call(bf16[128,768]{1,0:T(8,128)(2,1)} %get-tuple-element.32.refs_0_, bf16[128,768]{1,0:T(8,128)(2,1)} %copy-done.1, bf16[128,768]{1,0:T(8,128)(2,1)} %collective-permute-done.7.refs_2_, bf16[128,768]{1,0:T(8,128)(2,1)} %collective-permute-done.8.refs_3_), custom_call_target="tpu_custom_call" | custom-call | tf_op jit(solution)/shard_map/total/pallas_call | solution.py:192
Async XLA Ops:
  0.6 125.6 %copy-start = (bf16[64,1,32,768]{3,2,1,0:T(8,128)(2,1)S(1)}, bf16[64,1,32,768]{3,2,1,0:T(8,128)(2,1)}, u32[]{:S(2)}) copy-start(bf16[64,1,32,768]{3,2,1,0:T(8,128)(2,1)} %param.11) | copy-start | bytes 9437188
  3.2 51.5 %all-to-all-start = ((bf16[64,32,256]{2,1,0:T(8,128)(2,1)}), bf16[64,32,256]{2,1,0:T(8,128)(2,1)}, u32[]{:S(2)}, u32[]{:S(2)}) async-start(bf16[64,32,256]{2,1,0:T(8,128)(2,1)} %bitcast.29), calls=%async_computation | async-start | bytes 2097152 | tf_op jit(solution)/shard_map/all_to_all | solution.py:138
  27.5 14.2 %collective-permute-start.2 = (bf16[256,768]{1,0:T(8,128)(2,1)}, bf16[256,768]{1,0:T(8,128)(2,1)S(1)}, u32[]{:S(2)}, u32[]{:S(2)}) collective-permute-start(bf16[256,768]{1,0:T(8,128)(2,1)} %bitcast.38), channel_id=1, source_target_pairs={{0,192},{64,128},{128,64},{192,0},{256,448},{320,384},{384,320},{4... | collective-permute-start | bytes 1179656 | tf_op jit(solution)/shard_map/ppermute | solution.py:152
  31.4 18.6 %collective-permute-start.1 = (bf16[256,768]{1,0:T(8,128)(2,1)}, bf16[256,768]{1,0:T(8,128)(2,1)}, u32[]{:S(2)}, u32[]{:S(2)}) collective-permute-start(bf16[256,768]{1,0:T(8,128)(2,1)} %bitcast.39), channel_id=1, source_target_pairs={{0,128},{64,192},{128,0},{192,64},{256,384},{320,448},{384,256},{4... | collective-permute-start | bytes 1179656 | tf_op jit(solution)/shard_map/ppermute | solution.py:152
  33.6 16.4 %collective-permute-start = (bf16[256,768]{1,0:T(8,128)(2,1)}, bf16[256,768]{1,0:T(8,128)(2,1)}, u32[]{:S(2)}, u32[]{:S(2)}) collective-permute-start(bf16[256,768]{1,0:T(8,128)(2,1)} %bitcast.40), channel_id=1, source_target_pairs={{0,64},{64,0},{128,192},{192,128},{256,320},{320,256},{384,448},{4... | collective-permute-start | bytes 1179656 | tf_op jit(solution)/shard_map/ppermute | solution.py:152
  41.7 66.3 %copy-start.2 = (bf16[256,768]{1,0:T(8,128)(2,1)}, bf16[256,768]{1,0:T(8,128)(2,1)S(1)}, u32[]{:S(2)}) copy-start(bf16[256,768]{1,0:T(8,128)(2,1)S(1)} %collective-permute-done.2.refs_8_) | copy-start | bytes 1179652
  58.5 54.1 %collective-permute-start.3 = (bf16[8,64,256]{2,1,0:T(8,128)(2,1)}, bf16[8,64,256]{2,1,0:T(8,128)(2,1)}, u32[]{:S(2)}, u32[]{:S(2)}) collective-permute-start(bf16[8,64,256]{2,1,0:T(8,128)(2,1)} %get-tuple-element.25), channel_id=1, source_target_pairs={{0,64},{64,0},{128,192},{192,128},{256,320},{320,256},{384,448},{4... | collective-permute-start | bytes 786440 | tf_op jit(solution)/shard_map/ppermute | solution.py:152
  63.6 49.0 %collective-permute-start.4 = (bf16[8,64,256]{2,1,0:T(8,128)(2,1)}, bf16[8,64,256]{2,1,0:T(8,128)(2,1)}, u32[]{:S(2)}, u32[]{:S(2)}) collective-permute-start(bf16[8,64,256]{2,1,0:T(8,128)(2,1)} %get-tuple-element.26), channel_id=1, source_target_pairs={{0,128},{64,192},{128,0},{192,64},{256,384},{320,448},{384,256},{4... | collective-permute-start | bytes 786440 | tf_op jit(solution)/shard_map/ppermute | solution.py:152
  66.8 45.9 %collective-permute-start.5 = (bf16[8,64,256]{2,1,0:T(8,128)(2,1)}, bf16[8,64,256]{2,1,0:T(8,128)(2,1)}, u32[]{:S(2)}, u32[]{:S(2)}) collective-permute-start(bf16[8,64,256]{2,1,0:T(8,128)(2,1)} %get-tuple-element.27), channel_id=1, source_target_pairs={{0,192},{64,128},{128,64},{192,0},{256,448},{320,384},{384,320},{4... | collective-permute-start | bytes 786440 | tf_op jit(solution)/shard_map/ppermute | solution.py:152
  108.0 21.3 %all-to-all-start.3 = ((f32[64,1,256]{2,1,0:T(1,128)}), f32[64,1,256]{2,1,0:T(1,128)S(1)}, u32[]{:S(2)}, u32[]{:S(2)}) async-start(f32[64,1,256]{2,1,0:T(1,128)} %get-tuple-element.39), calls=%async_computation.3 | async-start | bytes 131072 | tf_op jit(solution)/shard_map/all_to_all | solution.py:210
  116.3 17.3 %collective-permute-start.6 = (bf16[128,768]{1,0:T(8,128)(2,1)}, bf16[128,768]{1,0:T(8,128)(2,1)S(1)}, u32[]{:S(2)}, u32[]{:S(2)}) collective-permute-start(bf16[128,768]{1,0:T(8,128)(2,1)} %get-tuple-element.33), channel_id=1, source_target_pairs={{0,256},{64,320},{128,384},{192,448},{256,512},{320,576},{384,640}... | collective-permute-start | bytes 589832 | tf_op jit(solution)/shard_map/ppermute | solution.py:190
  118.5 17.5 %collective-permute-start.7 = (bf16[128,768]{1,0:T(8,128)(2,1)}, bf16[128,768]{1,0:T(8,128)(2,1)}, u32[]{:S(2)}, u32[]{:S(2)}) collective-permute-start(bf16[128,768]{1,0:T(8,128)(2,1)} %get-tuple-element.34), channel_id=1, source_target_pairs={{0,512},{64,576},{128,640},{192,704},{256,768},{320,832},{384,896}... | collective-permute-start | bytes 589832 | tf_op jit(solution)/shard_map/ppermute | solution.py:190
  122.5 21.6 %collective-permute-start.8 = (bf16[128,768]{1,0:T(8,128)(2,1)}, bf16[128,768]{1,0:T(8,128)(2,1)}, u32[]{:S(2)}, u32[]{:S(2)}) collective-permute-start(bf16[128,768]{1,0:T(8,128)(2,1)} %get-tuple-element.35), channel_id=1, source_target_pairs={{0,768},{64,832},{128,896},{192,960},{256,0},{320,64},{384,128},{4... | collective-permute-start | bytes 589832 | tf_op jit(solution)/shard_map/ppermute | solution.py:190
  133.6 10.5 %copy-start.1 = (bf16[128,768]{1,0:T(8,128)(2,1)}, bf16[128,768]{1,0:T(8,128)(2,1)S(1)}, u32[]{:S(2)}) copy-start(bf16[128,768]{1,0:T(8,128)(2,1)S(1)} %collective-permute-done.6.refs_1_) | copy-start | bytes 589828

commit v4 on v3

--- a/solution.py
+++ b/solution.py
@@ -108,7 +108,7 @@
     spread = jnp.zeros((experts, tokens), F32)
     for k in range(top):
         spread = jnp.where(ids_ref[k : k + 1, :] == expert, grad[k : k + 1, :], spread)
-    term_ref[:, 0, :] = exact_dot(spread, input_ref[...].astype(F32))
+    term_ref[...] = exact_dot(spread, input_ref[...].astype(F32))
 
 
 def whole(shape, dtype):
@@ -204,10 +204,10 @@
     parts = lax.all_to_all(copies, "dp", 0, 0, tiled=True)
     logit_grad, term = pl.pallas_call(
         grad_kernel,
-        out_shape=(whole((top, tokens), F32), whole((experts, 1, dcols), F32)),
+        out_shape=(whole((top, tokens), F32), whole((experts, dcols), F32)),
         name="grads",
     )(parts, gating, ids, layer_input)
-    tiles = lax.all_to_all(term, "expert", 0, 0, tiled=True)
+    tiles = lax.all_to_all(term.reshape(n_expert, 1, dcols), "expert", 0, 0, tiled=True)
     router_grad = jnp.sum(tiles, axis=0)
     return (hidden_grad, down_grad.reshape(1, dcols, ff), logit_grad.T, router_grad)
 

time: 147 us -> 149 us (1.014)
  local copies, waits for them, and re-layouts: 0.02 us -> 1.55 us
    reshape x0 -> x1, local copies, waits for them, and re-layouts: none -> 1.53 us  [body(): term.reshape(n_expert, 1, dcols)]
  transfers between devices with their start and end apart: 11 -> 11, of which waited for: 6 -> 6; matrix products, arithmetic and copies ran while one was open for 4% -> 5% of each run, Pallas kernels for 5% -> 5%
where the time goes in v4:
time: 149 us; the launch traced here: 148 us
  starting transfers between devices  57.5 us (39%)
  blocking collectives  33.3 us (22%)
  waiting for transfers between devices  32.6 us (22%)
  Pallas kernels  15.9 us (11%)
  other arithmetic  3.14 us (2%)
  matrix products  3.12 us (2%)
  local copies, waits for them, and re-layouts  1.55 us (1%)
    all_to_all x1, starting transfers between devices, body(): lax.all_to_all(send.reshape(n_expert, capacity, dcols), 'expert', split_a...  24.2 us
    ppermute x6, starting transfers between devices, swapped(): return lax.ppermute(x, 'dp', [(i, i ^ p) for i in range(n_dp)])  18.8 us
    all_to_all x1, blocking collectives, body(): returned = lax.all_to_all(back[:, None, :], 'expert', 0, 0, tiled=True)  16.9 us
    all_to_all x1, blocking collectives, body(): parts = lax.all_to_all(copies, 'dp', 0, 0, tiled=True)  16.4 us
    ppermute x3, waiting for transfers between devices, body(): lax.ppermute(part[d], 'dp', [(i, (i + members * d) % n_dp) for i in range...  14.1 us
    ppermute x6, waiting for transfers between devices, swapped(): return lax.ppermute(x, 'dp', [(i, i ^ p) for i in range(n_dp)])  13.8 us
    ppermute x3, starting transfers between devices, body(): lax.ppermute(part[d], 'dp', [(i, (i + members * d) % n_dp) for i in range...  9.87 us
    all_to_all x1, waiting for transfers between devices, body(): lax.all_to_all(send.reshape(n_expert, capacity, dcols), 'expert', split_a...  4.76 us
  transfers between devices with their start and end apart: 11, of which 6 were waited for; matrix products, arithmetic and copies ran while one was open for 5% of the time, Pallas kernels for 5%

profile of v4, /device:TPU:1, one launch (start us, length us, event | category | flops | bytes accessed | tf_op | source)
XLA Modules:
  0.0 147.9 jit_solution(1902646459232060452)
XLA Ops:
  0.6 0.0 copy-start
  0.6 2.6 %place.1 = (bf16[2048,256]{1,0:T(8,128)(2,1)}, s32[64,128]{1,0:T(8,128)}, f32[8,128]{1,0:T(8,128)}) custom-call(s32[8,128]{1,0:T(8,128)} %bitcast.35, f32[8,128]{1,0:T(8,128)} %bitcast.38, bf16[128,256]{1,0:T(8,128)(2,1)} %refs_2_.1), custom_call_target="tpu_custom_call" | custom-call | tf_op jit(solution)/shard_map/place/pallas_call | solution.py:129
  3.2 24.2 %all-to-all-start = ((bf16[64,32,256]{2,1,0:T(8,128)(2,1)}), bf16[64,32,256]{2,1,0:T(8,128)(2,1)}, u32[]{:S(2)}, u32[]{:S(2)}) async-start(bf16[64,32,256]{2,1,0:T(8,128)(2,1)} %bitcast.30), calls=%async_computation | async-start | bytes 2097152 | tf_op jit(solution)/shard_map/all_to_all | solution.py:138
  27.5 4.0 %collective-permute-start.2 = (bf16[256,768]{1,0:T(8,128)(2,1)}, bf16[256,768]{1,0:T(8,128)(2,1)S(1)}, u32[]{:S(2)}, u32[]{:S(2)}) collective-permute-start(bf16[256,768]{1,0:T(8,128)(2,1)} %bitcast.40), channel_id=1, source_target_pairs={{0,192},{64,128},{128,64},{192,0},{256,448},{320,384},{384,320},{4... | collective-permute-start | bytes 1179656 | tf_op jit(solution)/shard_map/ppermute | solution.py:152
  31.4 2.2 %collective-permute-start.1 = (bf16[256,768]{1,0:T(8,128)(2,1)}, bf16[256,768]{1,0:T(8,128)(2,1)}, u32[]{:S(2)}, u32[]{:S(2)}) collective-permute-start(bf16[256,768]{1,0:T(8,128)(2,1)} %bitcast.41), channel_id=1, source_target_pairs={{0,128},{64,192},{128,0},{192,64},{256,384},{320,448},{384,256},{4... | collective-permute-start | bytes 1179656 | tf_op jit(solution)/shard_map/ppermute | solution.py:152
  33.6 2.1 %collective-permute-start = (bf16[256,768]{1,0:T(8,128)(2,1)}, bf16[256,768]{1,0:T(8,128)(2,1)}, u32[]{:S(2)}, u32[]{:S(2)}) collective-permute-start(bf16[256,768]{1,0:T(8,128)(2,1)} %bitcast.42), channel_id=1, source_target_pairs={{0,64},{64,0},{128,192},{192,128},{256,320},{320,256},{384,448},{4... | collective-permute-start | bytes 1179656 | tf_op jit(solution)/shard_map/ppermute | solution.py:152
  35.7 0.6 pad_add_fusion.refs_0_
  36.3 5.4 %collective-permute-done.2.refs_8_ = bf16[256,768]{1,0:T(8,128)(2,1)S(1)} collective-permute-done((bf16[256,768]{1,0:T(8,128)(2,1)}, bf16[256,768]{1,0:T(8,128)(2,1)S(1)}, u32[]{:S(2)}, u32[]{:S(2)}) %collective-permute-start.2) | collective-permute-done | bytes 393248 | tf_op jit(solution)/shard_map/ppermute | solution.py:152
  41.7 0.0 copy-start.2
  41.7 8.3 %collective-permute-done.1.refs_7_ = bf16[256,768]{1,0:T(8,128)(2,1)} collective-permute-done((bf16[256,768]{1,0:T(8,128)(2,1)}, bf16[256,768]{1,0:T(8,128)(2,1)}, u32[]{:S(2)}, u32[]{:S(2)}) %collective-permute-start.1) | collective-permute-done | bytes 393248 | tf_op jit(solution)/shard_map/ppermute | solution.py:152
  50.0 0.0 collective-permute-done.refs_6_
  50.0 4.8 %all-to-all-done.refs_1_ = bf16[64,32,256]{2,1,0:T(8,128)(2,1)} async-done(((bf16[64,32,256]{2,1,0:T(8,128)(2,1)}), bf16[64,32,256]{2,1,0:T(8,128)(2,1)}, u32[]{:S(2)}, u32[]{:S(2)}) %all-to-all-start) | async-done | bytes 1048608 | tf_op jit(solution)/shard_map/all_to_all | solution.py:138
  54.8 3.7 %turn.1 = (bf16[8,64,256]{2,1,0:T(8,128)(2,1)}, bf16[8,64,256]{2,1,0:T(8,128)(2,1)}, bf16[8,64,256]{2,1,0:T(8,128)(2,1)}, bf16[8,64,256]{2,1,0:T(8,128)(2,1)}) custom-call(s32[2]{0:T(128)} %pad_add_fusion.refs_0_, bf16[64,32,256]{2,1,0:T(8,128)(2,1)} %all-to-all-done.refs_1_), custom_call_target="tpu_custom_call" | custom-call | tf_op jit(solution)/shard_map/turn/pallas_call | solution.py:160
  58.5 5.1 %collective-permute-start.3 = (bf16[8,64,256]{2,1,0:T(8,128)(2,1)}, bf16[8,64,256]{2,1,0:T(8,128)(2,1)}, u32[]{:S(2)}, u32[]{:S(2)}) collective-permute-start(bf16[8,64,256]{2,1,0:T(8,128)(2,1)} %get-tuple-element.25), channel_id=1, source_target_pairs={{0,64},{64,0},{128,192},{192,128},{256,320},{320,256},{384,448},{4... | collective-permute-start | bytes 786440 | tf_op jit(solution)/shard_map/ppermute | solution.py:152
  63.6 3.1 %collective-permute-start.4 = (bf16[8,64,256]{2,1,0:T(8,128)(2,1)}, bf16[8,64,256]{2,1,0:T(8,128)(2,1)}, u32[]{:S(2)}, u32[]{:S(2)}) collective-permute-start(bf16[8,64,256]{2,1,0:T(8,128)(2,1)} %get-tuple-element.26), channel_id=1, source_target_pairs={{0,128},{64,192},{128,0},{192,64},{256,384},{320,448},{384,256},{4... | collective-permute-start | bytes 786440 | tf_op jit(solution)/shard_map/ppermute | solution.py:152
  66.8 2.3 %collective-permute-start.5 = (bf16[8,64,256]{2,1,0:T(8,128)(2,1)}, bf16[8,64,256]{2,1,0:T(8,128)(2,1)}, u32[]{:S(2)}, u32[]{:S(2)}) collective-permute-start(bf16[8,64,256]{2,1,0:T(8,128)(2,1)} %get-tuple-element.27), channel_id=1, source_target_pairs={{0,192},{64,128},{128,64},{192,0},{256,448},{320,384},{384,320},{4... | collective-permute-start | bytes 786440 | tf_op jit(solution)/shard_map/ppermute | solution.py:152
  69.1 1.9 %fusion = f32[64,32]{1,0:T(8,128)S(1)} fusion(bf16[64,32,256]{2,1,0:T(8,128)(2,1)} %all-to-all-done.refs_1_, bf16[64,1,32,256]{3,2,1,0:T(8,128)(2,1)} %param.12), kind=kLoop, calls=%fused_computation.1 | loop fusion | flops 2095104 | bytes 2105344 | tf_op jit(solution)/shard_map/reduce_sum | solution.py:156
  71.0 16.9 %all_to_all.20 = f32[64,1,32]{2,1,0:T(1,128)} all-to-all(f32[64,1,32]{2,1,0:T(1,128)S(1)} %bitcast.32), channel_id=1, replica_groups=mesh['dp'=16,'expert'=64] {'expert'}, dimensions={0} | all-to-all | bytes 16384 | tf_op jit(solution)/shard_map/all_to_all | solution.py:157
  87.9 1.9 %pick.1 = f32[16,8,128]{2,1,0:T(8,128)} custom-call(f32[64,32]{1,0:T(8,128)} %bitcast.33, s32[8,128]{1,0:T(8,128)} %bitcast.36, s32[64,128]{1,0:T(8,128)} %get-tuple-element.36.key_ref), custom_call_target="tpu_custom_call" | custom-call | tf_op jit(solution)/shard_map/pick/pallas_call | solution.py:201
  89.8 16.4 %all_to_all.21.parts_ref = f32[16,8,128]{2,1,0:T(8,128)} all-to-all(f32[16,8,128]{2,1,0:T(8,128)} %pick.1), channel_id=1, replica_groups=mesh['dp'=16,'expert'=64] {'dp'}, dimensions={0} | all-to-all | bytes 131072 | tf_op jit(solution)/shard_map/all_to_all | solution.py:204
  106.2 1.8 %grads.1 = (f32[8,128]{1,0:T(8,128)}, f32[64,256]{1,0:T(8,128)}) custom-call(f32[16,8,128]{2,1,0:T(8,128)} %all_to_all.21.parts_ref, f32[8,128]{1,0:T(8,128)} %get-tuple-element.37.gating_ref, s32[8,128]{1,0:T(8,128)} %bitcast.37, bf16[128,256]{1,0:T(8,128)(2,1)} %input_ref.1), custom_call_target="tpu_custom_call" | custom-call | tf_op jit(solution)/shard_map/grads/pallas_call | solution.py:205
  108.0 1.5 %copy.14 = f32[64,1,256]{2,1,0:T(1,128)} copy(f32[64,1,256]{2,0,1:T(8,128)} %bitcast.34) | data formatting | bytes 131072 | tf_op jit(solution)/shard_map/reshape | solution.py:210
  109.5 0.0 copy-done.2
  109.5 4.6 %all-to-all-start.3 = ((f32[64,1,256]{2,1,0:T(1,128)}), f32[64,1,256]{2,1,0:T(1,128)S(1)}, u32[]{:S(2)}, u32[]{:S(2)}) async-start(f32[64,1,256]{2,1,0:T(1,128)} %copy.14), calls=%async_computation.3 | async-start | bytes 131072 | tf_op jit(solution)/shard_map/all_to_all | solution.py:210
  114.1 0.0 collective-permute-done.3
  114.1 0.0 collective-permute-done.4
  114.1 0.0 collective-permute-done.5
  114.2 3.7 %hidden.1 = (bf16[128,768]{1,0:T(8,128)(2,1)}, bf16[128,768]{1,0:T(8,128)(2,1)}, bf16[128,768]{1,0:T(8,128)(2,1)}, bf16[128,768]{1,0:T(8,128)(2,1)}) custom-call(s32[2]{0:T(128)} %pad_add_fusion.refs_0_, bf16[512,256]{1,0:T(8,128)(2,1)} %bitcast.44, bf16[512,256]{1,0:T(8,128)(2,1)} %bitcast.7.refs_2_, bf16[512,256]{1,0:T(8,128)(2,1)} %bitcast.8.refs_3_, ...), custom_call_target="tpu_custom_call" | custom-call | flops 805306368 | bytes 1572864 | tf_op jit(solution)/shard_map/hidden/pallas_call | solution.py:175
  117.8 2.1 %collective-permute-start.6 = (bf16[128,768]{1,0:T(8,128)(2,1)}, bf16[128,768]{1,0:T(8,128)(2,1)S(1)}, u32[]{:S(2)}, u32[]{:S(2)}) collective-permute-start(bf16[128,768]{1,0:T(8,128)(2,1)} %get-tuple-element.33), channel_id=1, source_target_pairs={{0,256},{64,320},{128,384},{192,448},{256,512},{320,576},{384,640}... | collective-permute-start | bytes 589832 | tf_op jit(solution)/shard_map/ppermute | solution.py:190
  120.0 4.0 %collective-permute-start.7 = (bf16[128,768]{1,0:T(8,128)(2,1)}, bf16[128,768]{1,0:T(8,128)(2,1)}, u32[]{:S(2)}, u32[]{:S(2)}) collective-permute-start(bf16[128,768]{1,0:T(8,128)(2,1)} %get-tuple-element.34), channel_id=1, source_target_pairs={{0,512},{64,576},{128,640},{192,704},{256,768},{320,832},{384,896}... | collective-permute-start | bytes 589832 | tf_op jit(solution)/shard_map/ppermute | solution.py:190
  124.0 3.7 %collective-permute-start.8 = (bf16[128,768]{1,0:T(8,128)(2,1)}, bf16[128,768]{1,0:T(8,128)(2,1)}, u32[]{:S(2)}, u32[]{:S(2)}) collective-permute-start(bf16[128,768]{1,0:T(8,128)(2,1)} %get-tuple-element.35), channel_id=1, source_target_pairs={{0,768},{64,832},{128,896},{192,960},{256,0},{320,64},{384,128},{4... | collective-permute-start | bytes 589832 | tf_op jit(solution)/shard_map/ppermute | solution.py:190
  127.7 0.0 copy-done
  127.7 3.1 %convolution_bitcast_fusion = f32[1,256,768]{2,1,0:T(8,128)} fusion(bf16[2048,256]{1,0:T(8,128)(2,1)} %bitcast.12, bf16[2048,768]{1,0:T(8,128)(2,1)S(1)} %bitcast.29), kind=kOutput, calls=%fused_computation.2 | convolution fusion | flops 805306368 | bytes 4980736 | tf_op jit(solution)/shard_map/dot_general | solution.py:195
  130.8 0.0 all-to-all-done.3
  130.9 0.7 reduce_sum.21
  131.5 3.6 %collective-permute-done.6.refs_1_ = bf16[128,768]{1,0:T(8,128)(2,1)S(1)} collective-permute-done((bf16[128,768]{1,0:T(8,128)(2,1)}, bf16[128,768]{1,0:T(8,128)(2,1)S(1)}, u32[]{:S(2)}, u32[]{:S(2)}) %collective-permute-start.6) | collective-permute-done | bytes 196640 | tf_op jit(solution)/shard_map/ppermute | solution.py:190
  135.1 0.0 copy-start.1
  135.1 2.3 %collective-permute-done.7.refs_2_ = bf16[128,768]{1,0:T(8,128)(2,1)} collective-permute-done((bf16[128,768]{1,0:T(8,128)(2,1)}, bf16[128,768]{1,0:T(8,128)(2,1)}, u32[]{:S(2)}, u32[]{:S(2)}) %collective-permute-start.7) | collective-permute-done | bytes 196640 | tf_op jit(solution)/shard_map/ppermute | solution.py:190
  137.4 8.2 %collective-permute-done.8.refs_3_ = bf16[128,768]{1,0:T(8,128)(2,1)} collective-permute-done((bf16[128,768]{1,0:T(8,128)(2,1)}, bf16[128,768]{1,0:T(8,128)(2,1)}, u32[]{:S(2)}, u32[]{:S(2)}) %collective-permute-start.8) | collective-permute-done | bytes 196640 | tf_op jit(solution)/shard_map/ppermute | solution.py:190
  145.6 0.0 copy-done.1
  145.6 2.3 %total.1 = bf16[64,2,768]{2,1,0:T(2,128)(2,1)} custom-call(bf16[128,768]{1,0:T(8,128)(2,1)} %get-tuple-element.32.refs_0_, bf16[128,768]{1,0:T(8,128)(2,1)} %copy-done.1, bf16[128,768]{1,0:T(8,128)(2,1)} %collective-permute-done.7.refs_2_, bf16[128,768]{1,0:T(8,128)(2,1)} %collective-permute-done.8.refs_3_), custom_call_target="tpu_custom_call" | custom-call | tf_op jit(solution)/shard_map/total/pallas_call | solution.py:192
Async XLA Ops:
  0.6 127.1 %copy-start = (bf16[64,1,32,768]{3,2,1,0:T(8,128)(2,1)S(1)}, bf16[64,1,32,768]{3,2,1,0:T(8,128)(2,1)}, u32[]{:S(2)}) copy-start(bf16[64,1,32,768]{3,2,1,0:T(8,128)(2,1)} %param.11) | copy-start | bytes 9437188
  3.2 51.5 %all-to-all-start = ((bf16[64,32,256]{2,1,0:T(8,128)(2,1)}), bf16[64,32,256]{2,1,0:T(8,128)(2,1)}, u32[]{:S(2)}, u32[]{:S(2)}) async-start(bf16[64,32,256]{2,1,0:T(8,128)(2,1)} %bitcast.30), calls=%async_computation | async-start | bytes 2097152 | tf_op jit(solution)/shard_map/all_to_all | solution.py:138
  27.5 14.2 %collective-permute-start.2 = (bf16[256,768]{1,0:T(8,128)(2,1)}, bf16[256,768]{1,0:T(8,128)(2,1)S(1)}, u32[]{:S(2)}, u32[]{:S(2)}) collective-permute-start(bf16[256,768]{1,0:T(8,128)(2,1)} %bitcast.40), channel_id=1, source_target_pairs={{0,192},{64,128},{128,64},{192,0},{256,448},{320,384},{384,320},{4... | collective-permute-start | bytes 1179656 | tf_op jit(solution)/shard_map/ppermute | solution.py:152
  31.4 18.6 %collective-permute-start.1 = (bf16[256,768]{1,0:T(8,128)(2,1)}, bf16[256,768]{1,0:T(8,128)(2,1)}, u32[]{:S(2)}, u32[]{:S(2)}) collective-permute-start(bf16[256,768]{1,0:T(8,128)(2,1)} %bitcast.41), channel_id=1, source_target_pairs={{0,128},{64,192},{128,0},{192,64},{256,384},{320,448},{384,256},{4... | collective-permute-start | bytes 1179656 | tf_op jit(solution)/shard_map/ppermute | solution.py:152
  33.6 16.4 %collective-permute-start = (bf16[256,768]{1,0:T(8,128)(2,1)}, bf16[256,768]{1,0:T(8,128)(2,1)}, u32[]{:S(2)}, u32[]{:S(2)}) collective-permute-start(bf16[256,768]{1,0:T(8,128)(2,1)} %bitcast.42), channel_id=1, source_target_pairs={{0,64},{64,0},{128,192},{192,128},{256,320},{320,256},{384,448},{4... | collective-permute-start | bytes 1179656 | tf_op jit(solution)/shard_map/ppermute | solution.py:152
  41.7 67.8 %copy-start.2 = (bf16[256,768]{1,0:T(8,128)(2,1)}, bf16[256,768]{1,0:T(8,128)(2,1)S(1)}, u32[]{:S(2)}) copy-start(bf16[256,768]{1,0:T(8,128)(2,1)S(1)} %collective-permute-done.2.refs_8_) | copy-start | bytes 1179652
  58.5 55.6 %collective-permute-start.3 = (bf16[8,64,256]{2,1,0:T(8,128)(2,1)}, bf16[8,64,256]{2,1,0:T(8,128)(2,1)}, u32[]{:S(2)}, u32[]{:S(2)}) collective-permute-start(bf16[8,64,256]{2,1,0:T(8,128)(2,1)} %get-tuple-element.25), channel_id=1, source_target_pairs={{0,64},{64,0},{128,192},{192,128},{256,320},{320,256},{384,448},{4... | collective-permute-start | bytes 786440 | tf_op jit(solution)/shard_map/ppermute | solution.py:152
  63.6 50.5 %collective-permute-start.4 = (bf16[8,64,256]{2,1,0:T(8,128)(2,1)}, bf16[8,64,256]{2,1,0:T(8,128)(2,1)}, u32[]{:S(2)}, u32[]{:S(2)}) collective-permute-start(bf16[8,64,256]{2,1,0:T(8,128)(2,1)} %get-tuple-element.26), channel_id=1, source_target_pairs={{0,128},{64,192},{128,0},{192,64},{256,384},{320,448},{384,256},{4... | collective-permute-start | bytes 786440 | tf_op jit(solution)/shard_map/ppermute | solution.py:152
  66.8 47.4 %collective-permute-start.5 = (bf16[8,64,256]{2,1,0:T(8,128)(2,1)}, bf16[8,64,256]{2,1,0:T(8,128)(2,1)}, u32[]{:S(2)}, u32[]{:S(2)}) collective-permute-start(bf16[8,64,256]{2,1,0:T(8,128)(2,1)} %get-tuple-element.27), channel_id=1, source_target_pairs={{0,192},{64,128},{128,64},{192,0},{256,448},{320,384},{384,320},{4... | collective-permute-start | bytes 786440 | tf_op jit(solution)/shard_map/ppermute | solution.py:152
  109.5 21.3 %all-to-all-start.3 = ((f32[64,1,256]{2,1,0:T(1,128)}), f32[64,1,256]{2,1,0:T(1,128)S(1)}, u32[]{:S(2)}, u32[]{:S(2)}) async-start(f32[64,1,256]{2,1,0:T(1,128)} %copy.14), calls=%async_computation.3 | async-start | bytes 131072 | tf_op jit(solution)/shard_map/all_to_all | solution.py:210
  117.8 17.3 %collective-permute-start.6 = (bf16[128,768]{1,0:T(8,128)(2,1)}, bf16[128,768]{1,0:T(8,128)(2,1)S(1)}, u32[]{:S(2)}, u32[]{:S(2)}) collective-permute-start(bf16[128,768]{1,0:T(8,128)(2,1)} %get-tuple-element.33), channel_id=1, source_target_pairs={{0,256},{64,320},{128,384},{192,448},{256,512},{320,576},{384,640}... | collective-permute-start | bytes 589832 | tf_op jit(solution)/shard_map/ppermute | solution.py:190
  120.0 17.5 %collective-permute-start.7 = (bf16[128,768]{1,0:T(8,128)(2,1)}, bf16[128,768]{1,0:T(8,128)(2,1)}, u32[]{:S(2)}, u32[]{:S(2)}) collective-permute-start(bf16[128,768]{1,0:T(8,128)(2,1)} %get-tuple-element.34), channel_id=1, source_target_pairs={{0,512},{64,576},{128,640},{192,704},{256,768},{320,832},{384,896}... | collective-permute-start | bytes 589832 | tf_op jit(solution)/shard_map/ppermute | solution.py:190
  124.0 21.6 %collective-permute-start.8 = (bf16[128,768]{1,0:T(8,128)(2,1)}, bf16[128,768]{1,0:T(8,128)(2,1)}, u32[]{:S(2)}, u32[]{:S(2)}) collective-permute-start(bf16[128,768]{1,0:T(8,128)(2,1)} %get-tuple-element.35), channel_id=1, source_target_pairs={{0,768},{64,832},{128,896},{192,960},{256,0},{320,64},{384,128},{4... | collective-permute-start | bytes 589832 | tf_op jit(solution)/shard_map/ppermute | solution.py:190
  135.1 10.5 %copy-start.1 = (bf16[128,768]{1,0:T(8,128)(2,1)}, bf16[128,768]{1,0:T(8,128)(2,1)S(1)}, u32[]{:S(2)}) copy-start(bf16[128,768]{1,0:T(8,128)(2,1)S(1)} %collective-permute-done.6.refs_1_) | copy-start | bytes 589828
